TPU v7x, 32 devices: a whole 2x2x4 slice. The times are simulated.
32 devices in a mesh: dp: 16 (over z, y, x), stream: 2 (over core).
Axes of the slice: x: 2, y: 2, z: 4, core: 2. Of those that a mesh axis runs over, the one named last changes fastest.
Arguments:
- residual: bfloat16 [32768, 1024], P(('dp', 'stream')), may hold values from -6 to 6
- cotangent: bfloat16 [32768, 1024], P(('dp', 'stream')), may hold values from -6 to 6
- ln_gain: bfloat16 [1024], replicated, may hold values from 0.5 to 1.5
- ln_bias: bfloat16 [1024], replicated, may hold values from -1.25 to 1.25
- w_qkv: bfloat16 [1024, 3072], replicated, may hold values from -0.1875 to 0.1875
- b_qkv: bfloat16 [3072], replicated, may hold values from -1.25 to 1.25
- w_proj: bfloat16 [1024, 1024], replicated, may hold values from -0.375 to 0.375
- b_proj: bfloat16 [1024], replicated, may hold values from -1.25 to 1.25
- feature_scale: bfloat16 [1024], replicated, may hold values from 0.5 to 2
- w_up: bfloat16 [1024, 4096], replicated, may hold values from -0.1875 to 0.1875
- b_up: bfloat16 [4096], replicated, may hold values from -1.25 to 1.25
- w_down: bfloat16 [4096, 1024], replicated, may hold values from -0.09375 to 0.09375
- b_down: bfloat16 [1024], replicated, may hold values from -1.25 to 1.25
- qmc_points: float32 [64, 64], replicated, may hold values from -5 to 5
- slot_lengths: int32 [16], P('dp'), may hold values from 128 to 2048, as said below
Outputs:
- block_out: bfloat16 [32768, 1024], P(('dp', 'stream'))
- residual_grad: float32 [32768, 1024], P(('dp', 'stream'))
- gain_grad: float32 [1024], P(('dp', 'stream'))
- shift_grad: float32 [1024], P(('dp', 'stream'))
- qkvw_grad: float32 [1024, 3072], P(('dp', 'stream'))
- qkvb_grad: float32 [3072], P(('dp', 'stream'))
- projw_grad: float32 [1024, 1024], P(('dp', 'stream'))
- projb_grad: float32 [1024], P(('dp', 'stream'))
- scale_grad: float32 [1024], P(('dp', 'stream'))
- upw_grad: float32 [1024, 4096], P(('dp', 'stream'))
- upb_grad: float32 [4096], P(('dp', 'stream'))
- downw_grad: float32 [4096, 1024], P(('dp', 'stream'))
- downb_grad: float32 [1024], P(('dp', 'stream'))
Inputs may be any that keep to these rules, and one draw needn't show every extreme that they name: Slot j holds one sequence at its first slot_lengths[j] positions; the rest of its 2048 positions is padding. The least and the largest length occur in every draw.
All inputs are finite; a program needn't handle non-finite values.
Results may differ from a plain program's by a relative error of at most 0.0093.
Values may be sent and summed in bfloat16 or wider, within the bound.
No kernel may reach another device: no remote copies, remote signals or barrier semaphores. Data moves between devices by JAX's collectives and lax.ppermute only.
A program may use at most 384 MiB of HBM per device.

v0:
```python
from functools import partial
import math

import jax
import jax.numpy as jnp
import numpy as np
from jax import lax
from jax.experimental import pallas as pl
from jax.experimental.pallas import tpu as pltpu
from jax.sharding import PartitionSpec as P

HEAD = 64
ROT = 16
LEN = 2048
EPSILON = 1e-05

BF = jnp.bfloat16
F32 = jnp.float32
TILE = 256
CHUNK = 128
GROUP = 256
PACK = GROUP // HEAD
LANES = 128
ERFC = tuple(
    item * math.sqrt(0.5 * math.pi)
    for item in (0.254829592, -0.284496736, 1.421413741, -1.453152027, 1.061405429)
)
VMEM_CAP = 55 * 1024 * 1024

NN = (((1,), (0,)), ((), ()))
NT = (((1,), (1,)), ((), ()))
TN = (((0,), (0,)), ((), ()))


def mm(left, right, dims=NN):
    return lax.dot_general(left, right, dims, preferred_element_type=F32)


def split(value):
    high = value.astype(BF)
    return high, (value - high.astype(F32)).astype(BF)


def whole(shape):
    rank = len(shape)
    return pl.BlockSpec(shape, lambda *_: (0,) * rank, pipeline_mode=pl.Buffered(1))


def anywhere():
    return pl.BlockSpec(memory_space=pl.ANY)


def params(limit=VMEM_CAP):
    return pltpu.CompilerParams(vmem_limit_bytes=limit)


def vector_spec(width, at, side=None):
    return pl.BlockSpec(
        (1, width),
        lambda i, info: (0, at // width + (0 if side is None else info[0])),
        pipeline_mode=pl.Buffered(1),
    )


def cost(flops, moved, trans=0):
    return pl.CostEstimate(flops=int(0.4 * flops), bytes_accessed=int(0.4 * moved), transcendentals=int(0.4 * trans))


def exact_row(row, weights):
    high, low = split(jnp.broadcast_to(row, (8, row.shape[1])))
    both = mm(jnp.concatenate([high, low], axis=0), weights, NT)
    return both[0:1] + both[8:9]


def norm_stats(rows):
    mean = jnp.mean(rows, axis=-1, keepdims=True)
    centred = rows - mean
    rstd = lax.rsqrt(jnp.mean(centred * centred, axis=-1, keepdims=True) + EPSILON)
    return centred * rstd, rstd


def strip_copy(side, source, buf, sems, kind, j):
    there = pl.ds(pl.multiple_of((2 * j + side) * LANES, LANES), LANES)
    here = pl.ds(pl.multiple_of(j * LANES, LANES), LANES)
    if kind == 0:
        return pltpu.make_async_copy(source.at[:, there], buf.at[:, here], sems.at[kind, j])
    return pltpu.make_async_copy(source.at[there, :], buf.at[here, :], sems.at[kind, j])


def part_copy(side, source, buf, sems, p):
    width = buf.shape[1] // 3
    there = pl.ds(pl.multiple_of((2 * p + side) * width, LANES), width)
    return pltpu.make_async_copy(source.at[:, there], buf.at[:, p * width : (p + 1) * width], sems.at[p])


def mlp_kernel(half, tiles, info, res, cot, gain, bias, b_up, w_up, w_down, *rest):
    normed, target, act, up_grad, upb, sums, up_buf, down_buf, sems = rest[-9:]
    step = pl.program_id(0)
    side = info[0]

    @pl.when(step == 0)
    def _():
        @pl.loop(0, up_buf.shape[1] // LANES)
        def _(j):
            strip_copy(side, w_up, up_buf, sems, 0, j).start()
            strip_copy(side, w_down, down_buf, sems, 1, j).start()

        if half == 0:
            upb[...] = jnp.zeros_like(upb)
            sums[...] = jnp.zeros_like(sums)
        else:
            upb[...] = rest[4][...]

    rows = res.shape[0]
    xhat, _ = norm_stats(res[...].astype(F32))
    low = (xhat * gain[...] + bias[...]).astype(BF)
    normed[...] = low
    part = side if half == 0 else 1 - side
    place = (part * tiles + step) * rows + lax.broadcasted_iota(jnp.int32, (rows, 1), 0)
    tgt = jnp.where(place < info[2], cot[...], jnp.zeros_like(cot))
    target[...] = tgt
    ones = jnp.ones((8, rows), BF)
    if half == 0:
        sums[...] += mm(ones, tgt)[0:1]
    width = 1024
    strips = width // LANES

    @pl.loop(0, up_buf.shape[1] // width)
    def _(j):
        cols = pl.ds(pl.multiple_of(j * width, width), width)

        @pl.when(step == 0)
        def _():
            for b in range(strips):
                strip_copy(side, w_up, up_buf, sems, 0, j * strips + b).wait()
                strip_copy(side, w_down, down_buf, sems, 1, j * strips + b).wait()

        shift = jnp.concatenate(
            [
                b_up[:, pl.ds(pl.multiple_of((2 * (j * strips + b) + side) * LANES, LANES), LANES)]
                for b in range(strips)
            ],
            axis=1,
        )
        up = mm(low, up_buf[:, cols]) + shift
        back = mm(tgt, down_buf[cols, :], NT)
        bell = jnp.exp2(up * up * (-0.5 * math.log2(math.e)) - 0.5 * math.log2(2.0 * math.pi))
        t = 1.0 / (1.0 + (0.3275911 * math.sqrt(0.5)) * jnp.abs(up))
        poly = ERFC[4]
        for item in ERFC[3::-1]:
            poly = item + t * poly
        tail = (t * bell) * poly
        phi = jnp.where(up >= 0, 1.0 - tail, tail)
        act[:, cols] = (up * phi).astype(BF)
        grad = (back * (phi + up * bell)).astype(BF)
        up_grad[:, cols] = grad
        upb[:, cols] += mm(ones, grad)[0:1]

    if half == 1:

        @pl.when(step == tiles - 1)
        def _():
            sums[...] = jnp.zeros_like(sums)

            @pl.loop(0, upb.shape[1] // GROUP)
            def _(j):
                cols = pl.ds(pl.multiple_of(j * GROUP, GROUP), GROUP)
                sums[...] += exact_row(upb[:, cols], up_buf[:, cols])


def mlp_rows(half, info, res, cot, vectors, w_up, w_down, earlier=()):
    rows, dim = res.shape
    ff = w_up.shape[1] // 2
    tiles = rows // TILE
    total = 2 * rows
    shift = half * tiles
    row_map = lambda i, info: (i, 0)
    out_map = lambda i, info: (i + shift, 0)
    outs = (
        jax.ShapeDtypeStruct((total, dim), BF),
        jax.ShapeDtypeStruct((total, dim), BF),
        jax.ShapeDtypeStruct((total, ff), BF),
        jax.ShapeDtypeStruct((total, ff), BF),
        jax.ShapeDtypeStruct((1, ff), F32),
        jax.ShapeDtypeStruct((1, dim), F32),
    )
    return pl.pallas_call(
        partial(mlp_kernel, half, tiles),
        out_shape=outs,
        grid_spec=pltpu.PrefetchScalarGridSpec(
            num_scalar_prefetch=1,
            grid=(tiles,),
            in_specs=[
                pl.BlockSpec((TILE, dim), row_map),
                pl.BlockSpec((TILE, dim), row_map),
                vector_spec(dim, 0),
                vector_spec(dim, dim),
                vector_spec(2 * ff, 8 * dim),
                anywhere(),
                anywhere(),
            ]
            + [anywhere()] * (len(earlier) - 1)
            + [whole((1, ff))] * min(len(earlier), 1),
            out_specs=[
                pl.BlockSpec((TILE, dim), out_map),
                pl.BlockSpec((TILE, dim), out_map),
                pl.BlockSpec((TILE, ff), out_map),
                pl.BlockSpec((TILE, ff), out_map),
                whole((1, ff)),
                whole((1, dim)),
            ],
            scratch_shapes=[
                pltpu.VMEM((dim, ff), BF),
                pltpu.VMEM((ff, dim), BF),
                pltpu.SemaphoreType.DMA((2, ff // LANES)),
            ],
        ),
        input_output_aliases={8 + j: j for j in range(len(earlier) - 1)},
        compiler_params=params(63 * 1024 * 1024),
        cost_estimate=cost(4 * rows * dim * ff, 12 * rows * dim + 16 * rows * ff, 2 * rows * ff),
        name="mlp_rows",
    )(info, res, cot, vectors, vectors, vectors, w_up, w_down, *earlier)


def ship(table, which, buf, send, keep, sems, first, count):
    half = send.shape[0]
    for b in range(count):
        spot = table[which, first + b]

        @pl.when(spot >= half)
        def _():
            pltpu.make_async_copy(buf.at[first + b], send.at[spot - half], sems.at[first + b]).start()

        @pl.when(spot < half)
        def _():
            pltpu.make_async_copy(buf.at[first + b], keep.at[spot], sems.at[first + b]).start()


def shipped(buf, keep, sems):
    for b in range(buf.shape[0]):
        pltpu.make_async_copy(buf.at[b], keep.at[0], sems.at[b]).wait()


def mlp_grad_kernel(
    tiles, table, act, target, normed, up_grad, send_a, keep_a, send_b, keep_b,
    grads, buf_a, buf_b, sems_a, sems_b, sem,
):
    step = pl.program_id(0)

    @pl.when(step == 0)
    def _():
        pltpu.make_async_copy(up_grad, grads, sem).start()

    @pl.when(step < tiles)
    def _():
        value = mm(act[...], target[...], TN).astype(BF)
        size = buf_a.shape[1]
        count = value.shape[0] // size
        first = step * count
        for b in range(count):
            buf_a[first + b] = value[b * size : (b + 1) * size, :]
        ship(table, 0, buf_a, send_a, keep_a, sems_a, first, count)

    @pl.when(step == tiles)
    def _():
        pltpu.make_async_copy(up_grad, grads, sem).wait()

    @pl.when(step >= tiles)
    def _():
        value = mm(normed[...], grads[...], TN).astype(BF)
        size = buf_b.shape[1] // 2
        width = buf_b.shape[2]
        count = value.shape[0] // size
        first = (step - tiles) * count
        for b in range(count):
            for p in range(2):
                buf_b[first + b, p * size : (p + 1) * size, :] = value[
                    b * size : (b + 1) * size, p * width : (p + 1) * width
                ]
        ship(table, 1, buf_b, send_b, keep_b, sems_b, first, count)

    @pl.when(step == pl.num_programs(0) - 1)
    def _():
        shipped(buf_a, keep_a, sems_a)
        shipped(buf_b, keep_b, sems_b)


def mlp_weight_grads(ndp, table, act, target, normed, up_grad):
    total, dim = normed.shape
    ff = act.shape[1]
    rows = ff // ndp
    shape = jax.ShapeDtypeStruct((ndp // 2, rows, dim), BF)
    wide, narrow = 512, 256
    tiles = ff // wide
    return pl.pallas_call(
        partial(mlp_grad_kernel, tiles),
        out_shape=(shape,) * 4,
        grid_spec=pltpu.PrefetchScalarGridSpec(
            num_scalar_prefetch=1,
            grid=(tiles + dim // narrow,),
            in_specs=[
                pl.BlockSpec((total, wide), lambda i, t: (0, jnp.minimum(i, tiles - 1))),
                whole((total, dim)),
                pl.BlockSpec((total, narrow), lambda i, t: (0, jnp.maximum(i - tiles, 0))),
                anywhere(),
            ],
            out_specs=[anywhere()] * 4,
            scratch_shapes=[pltpu.VMEM((total, ff), BF)]
            + [pltpu.VMEM((ndp, rows, dim), BF)] * 2
            + [pltpu.SemaphoreType.DMA((ndp,))] * 2
            + [pltpu.SemaphoreType.DMA],
        ),
        compiler_params=params(),
        cost_estimate=cost(4 * total * dim * ff, 4 * total * (dim + ff) + 4 * dim * ff),
        name="mlp_weight_grads",
    )(table, act, target, normed, up_grad)


def attn_grad_kernel(
    table, normed, attended, target, dq, dk, dv, extra, send_a, keep_a, send_b, keep_b, buf_a, buf_b, sems_a, sems_b
):
    step = pl.program_id(0)
    ndp = buf_a.shape[0]
    size = buf_a.shape[1] // 2
    small = size // 2
    half = dq.shape[1]

    @pl.when(step == 0)
    def _():
        value = mm(attended[...], target[...], TN).astype(BF)
        for b in range(ndp):
            for p in range(2):
                at = size + p * small
                buf_b[b, at : at + small, :] = value[b * small : (b + 1) * small, p * half : (p + 1) * half]
            buf_b[b, 2 * size :, :] = extra[b]

    count = normed.shape[1] // size
    first = step * count
    for item, buf, at in ((dq, buf_a, 0), (dk, buf_a, size), (dv, buf_b, 0)):
        value = mm(normed[...], item[...], TN).astype(BF)
        for b in range(count):
            buf[first + b, at : at + size, :] = value[b * size : (b + 1) * size, :]
    ship(table, 0, buf_a, send_a, keep_a, sems_a, first, count)
    ship(table, 1, buf_b, send_b, keep_b, sems_b, first, count)

    @pl.when(step == pl.num_programs(0) - 1)
    def _():
        shipped(buf_a, keep_a, sems_a)
        shipped(buf_b, keep_b, sems_b)


def attn_weight_grads(ndp, table, normed, target, attended, dq, dk, dv, extra):
    total, dim = normed.shape
    half = dq.shape[1]
    rows = 2 * dim // ndp
    more = extra.shape[1]
    shapes = [jax.ShapeDtypeStruct((ndp // 2, rows + j * more, half), BF) for j in range(2)]
    step = 256
    return pl.pallas_call(
        attn_grad_kernel,
        out_shape=(shapes[0], shapes[0], shapes[1], shapes[1]),
        grid_spec=pltpu.PrefetchScalarGridSpec(
            num_scalar_prefetch=1,
            grid=(dim // step,),
            in_specs=[
                pl.BlockSpec((total, step), lambda i, t: (0, i)),
                whole((total, half)),
                whole((total, dim)),
            ]
            + [whole((total, half))] * 3
            + [whole(extra.shape)],
            out_specs=[anywhere()] * 4,
            scratch_shapes=[pltpu.VMEM((ndp, rows + j * more, half), BF) for j in range(2)]
            + [pltpu.SemaphoreType.DMA((ndp,))] * 2,
        ),
        compiler_params=params(),
        cost_estimate=cost(8 * total * dim * half, 2 * total * (2 * dim + 4 * half) + 8 * dim * half),
        name="attn_weight_grads",
    )(table, normed, attended, target, dq, dk, dv, extra)


def turn(value, cosine, sine_low, sine_high):
    pieces = []
    for j in range(value.shape[1] // LANES):
        item = value[:, j * LANES : (j + 1) * LANES]
        pieces.append(
            item * cosine
            + pltpu.roll(item, LANES - ROT // 2, 1) * sine_low
            + pltpu.roll(item, ROT // 2, 1) * sine_high
        )
    return jnp.concatenate(pieces, axis=1)


def patterns():
    row_head = lax.broadcasted_iota(jnp.int32, (PACK * CHUNK, GROUP), 0) // CHUNK
    lane_head = lax.broadcasted_iota(jnp.int32, (PACK * CHUNK, GROUP), 1) // HEAD
    block_row = lax.broadcasted_iota(jnp.int32, (GROUP, GROUP), 0) // HEAD
    block_col = lax.broadcasted_iota(jnp.int32, (GROUP, GROUP), 1) // HEAD
    return row_head == lane_head, block_row == block_col


def interleave(items, lag):
    waiting = [(j * lag, item) for j, item in enumerate(items)]
    at = 0
    while waiting:
        alive = []
        for begin, item in waiting:
            if at < begin or next(item, waiting) is not waiting:
                alive.append((begin, item))
        waiting = alive
        at += 1


def stack(mask, item):
    return jnp.where(mask, jnp.concatenate([item] * PACK, axis=0), jnp.zeros((), BF))


def sum_heads(item, ones):
    high, low = split(item)
    return mm(high, ones) + mm(low, ones)


def tables(coarse, fine, tile):
    rows = TILE // 8
    co, so = [], []
    outer = coarse[pl.ds(tile * rows, rows)]
    ci, si = fine[0:8, :][None], fine[8:16, :][None]
    co, so = outer[:, 0:1, :], outer[:, 1:2, :]
    flat = lambda item: item.reshape(TILE, LANES)
    cosine = flat(co * ci - so * si)
    sine = so * ci + co * si
    return cosine, flat(sine * fine[16:24, :][None]), flat(sine * fine[24:32, :][None])


def attn_front_kernel(
    info, normed, target, w_q, w_k, w_v, b_q, b_k, b_v, w_proj, scale, mix_high, mix_low, base, inner,
    attended, dq, fq_s, fk_s, v_s, tk_s, gn_s, gx_s, bias_q, scale_grad, state, total,
):
    step = pl.program_id(0)
    groups = w_q.shape[1] // GROUP
    span = TILE // CHUNK
    stack_mask, block_mask = patterns()
    ones = jnp.where(block_mask, 1.0, 0.0).astype(BF)
    causal = lax.broadcasted_iota(jnp.int32, (CHUNK, PACK * CHUNK), 0) >= (
        lax.broadcasted_iota(jnp.int32, (CHUNK, PACK * CHUNK), 1) % CHUNK
    )
    lower = jnp.where(
        lax.broadcasted_iota(jnp.int32, (CHUNK, CHUNK), 0) >= lax.broadcasted_iota(jnp.int32, (CHUNK, CHUNK), 1),
        1.0,
        0.0,
    ).astype(BF)

    @pl.when(step == 0)
    def _():
        for item in (state, total, bias_q, scale_grad):
            item[...] = jnp.zeros_like(item)

    x = normed[...]
    cosine, low, high = tables(base, inner, step)
    grad_all = mm(target[...], w_proj[...], NT)
    feats, turned, values, held, before = {}, {}, {}, {}, {}

    def feature(g, which):
        cols = slice(g * GROUP, (g + 1) * GROUP)
        w, b, out = ((w_q, b_q, fq_s), (w_k, b_k, fk_s))[which]
        t = mm(x, w[:, cols]) + b[:, cols]
        yield
        t = turn(t, cosine, low, high)
        turned[which, g] = t
        t_high, t_low = split(t)
        spread = mm(t_high, mix_high[...]) + mm(t_low, mix_high[...]) + mm(t_high, mix_low[...])
        yield
        square = sum_heads(t * t, ones)
        yield
        feats[which, g] = (scale[:, cols] * jnp.exp(spread - square * (0.5 * HEAD ** (-0.5)))).astype(BF)
        out[:, cols] = feats[which, g]
        if which == 1:
            tk_s[:, cols] = t.astype(BF)
            values[g] = (mm(x, w_v[:, cols]) + b_v[:, cols]).astype(BF)
            v_s[:, cols] = values[g]
        yield

    def unit(g, c):
        cols = slice(g * GROUP, (g + 1) * GROUP)
        rows = slice(c * CHUNK, (c + 1) * CHUNK)
        fq, fk, vc = feats[0, g][rows], feats[1, g][rows], values[g][rows]
        stack_k, stack_v = stack(stack_mask, fk), stack(stack_mask, vc)
        kept = state[g]
        held = kept.astype(BF)
        state[g] = kept + jnp.where(block_mask, mm(fk, vc, TN), 0.0)
        keys = mm(lower, fk) + total[g]
        total[g] = keys[CHUNK - 1 : CHUNK, :]
        yield
        weight = jnp.where(causal, mm(fq, stack_k, NT), 0.0).astype(BF)
        wide = fq.astype(F32)
        den = sum_heads(wide * keys, ones)
        yield
        num = mm(weight, stack_v) + mm(fq, held)
        inverse = 1.0 / den
        yield
        mixed = num * inverse
        attended[rows, cols] = mixed.astype(BF)
        gn = (grad_all[rows, cols] * inverse).astype(BF)
        gn_s[rows, cols] = gn
        edge = jnp.where(causal, mm(gn, stack_v, NT), 0.0).astype(BF)
        yield
        grad_den = -sum_heads(gn.astype(F32) * mixed, ones)
        gx_s[rows, cols] = (grad_den * wide).astype(BF)
        yield
        dfq = mm(edge, stack_k) + mm(gn, held, NT) + grad_den * keys
        back = dfq * wide
        back_low = back.astype(BF)
        scale_grad[:, cols] += jnp.sum(back, axis=0, keepdims=True)
        yield
        dt = mm(back_low, mix_high[...], NT) + mm(back_low, mix_low[...], NT)
        dt = dt - mm(back_low, ones) * turned[0, g][rows] * (HEAD ** (-0.5))
        yield
        out = turn(dt, cosine[rows], -low[rows], -high[rows]).astype(BF)
        dq[rows, cols] = out
        bias_q[:, cols] += jnp.sum(out.astype(F32), axis=0, keepdims=True)
        yield

    interleave([feature(g, which) for g in range(groups) for which in range(2)], 0)
    interleave([unit(g, c) for c in range(span) for g in range(groups)], 0)


def attn_rear_kernel(
    tiles, info, fq_s, fk_s, v_s, tk_s, gn_s, gx_s, mix_high, mix_low, base, inner, bias_in, scale_in, scale,
    w_qkv, shift_in, dk, dv, sums_out, shift_out, bias_k, bias_v, scale_grad, w_buf, sems, state, total,
):
    step = pl.program_id(0)
    tile = tiles - 1 - step
    groups = dk.shape[1] // GROUP
    span = TILE // CHUNK
    stack_mask, block_mask = patterns()
    ones = jnp.where(block_mask, 1.0, 0.0).astype(BF)
    causal = lax.broadcasted_iota(jnp.int32, (CHUNK, PACK * CHUNK), 1) % CHUNK >= (
        lax.broadcasted_iota(jnp.int32, (CHUNK, PACK * CHUNK), 0)
    )
    upper = jnp.where(
        lax.broadcasted_iota(jnp.int32, (CHUNK, CHUNK), 1) >= lax.broadcasted_iota(jnp.int32, (CHUNK, CHUNK), 0),
        1.0,
        0.0,
    ).astype(BF)

    @pl.when(step == 0)
    def _():
        for item in (state, total, bias_k, bias_v):
            item[...] = jnp.zeros_like(item)
        for p in range(3):
            part_copy(info[0], w_qkv, w_buf, sems, p).start()
        scale_grad[...] = scale_in[...]

    cosine, low, high = tables(base, inner, tile)

    def unit(g, c):
        cols = slice(g * GROUP, (g + 1) * GROUP)
        rows = slice(c * CHUNK, (c + 1) * CHUNK)
        fq, fk, vc, gn = fq_s[rows, cols], fk_s[rows, cols], v_s[rows, cols], gn_s[rows, cols]
        stack_q, stack_g = stack(stack_mask, fq), stack(stack_mask, gn)
        kept = state[g]
        held = kept.astype(BF)
        state[g] = kept + jnp.where(block_mask, mm(fq, gn, TN), 0.0)
        sums = mm(upper, gx_s[rows, cols]) + total[g]
        total[g] = sums[0:1, :]
        yield
        edge = jnp.where(causal, mm(vc, stack_g, NT), 0.0).astype(BF)
        yield
        weight = jnp.where(causal, mm(fk, stack_q, NT), 0.0).astype(BF)
        yield
        dfk = mm(edge, stack_q) + mm(vc, held, NT) + sums
        back = dfk * fk.astype(F32)
        back_low = back.astype(BF)
        scale_grad[:, cols] += jnp.sum(back, axis=0, keepdims=True)
        yield
        dvc = (mm(weight, stack_g) + mm(fk, held)).astype(BF)
        dv[rows, cols] = dvc
        bias_v[:, cols] += jnp.sum(dvc.astype(F32), axis=0, keepdims=True)
        yield
        dt = mm(back_low, mix_high[...], NT) + mm(back_low, mix_low[...], NT)
        dt = dt - mm(back_low, ones) * tk_s[rows, cols].astype(F32) * (HEAD ** (-0.5))
        yield
        out = turn(dt, cosine[rows], -low[rows], -high[rows]).astype(BF)
        dk[rows, cols] = out
        bias_k[:, cols] += jnp.sum(out.astype(F32), axis=0, keepdims=True)
        yield

    interleave([unit(g, c) for c in reversed(range(span)) for g in range(groups)], 1)

    @pl.when(step == tiles - 1)
    def _():
        sums_out[0:1, :] = bias_in[...]
        sums_out[1:2, :] = bias_k[...]
        sums_out[2:3, :] = bias_v[...]
        sums_out[3:4, :] = scale_grad[...] / scale[...]
        shift_out[...] = shift_in[...]
        for p in range(3):
            part_copy(info[0], w_qkv, w_buf, sems, p).wait()

        @pl.loop(0, 3 * groups)
        def _(j):
            row = sums_out[pl.ds(j // groups, 1), pl.ds(pl.multiple_of((j % groups) * GROUP, GROUP), GROUP)]
            shift_out[...] += exact_row(row, w_buf[:, pl.ds(pl.multiple_of(j * GROUP, GROUP), GROUP)])


def turn_tables():
    lane = np.arange(LANES) % HEAD
    freqs = np.where(lane < ROT, 10000.0 ** (-(lane % (ROT // 2)) / (ROT // 2)), 0.0)
    waves = lambda places: np.stack([np.cos(places[:, None] * freqs), np.sin(places[:, None] * freqs)], axis=1)
    fine = np.concatenate(
        [
            waves(np.arange(8)).transpose(1, 0, 2).reshape(16, LANES),
            np.broadcast_to(np.where(lane < ROT // 2, -1.0, 0.0), (8, LANES)),
            np.broadcast_to(np.where((lane >= ROT // 2) & (lane < ROT), 1.0, 0.0), (8, LANES)),
        ]
    )
    return waves(np.arange(LEN // 8) * 8.0).astype(np.float32), fine.astype(np.float32)


def prepare_kernel(*refs):
    *parts, points, basis, vectors, mix_high, mix_low = refs
    at = 0
    for part in parts:
        count = part.shape[0]
        vectors[:, at : at + count] = part[...].astype(F32).reshape(1, count)
        at += count
    table = jnp.dot(basis[...], points[...], precision=lax.Precision.HIGHEST, preferred_element_type=F32)
    wide = jnp.concatenate([table] * PACK, axis=1)
    _, block_mask = patterns()
    tall = jnp.where(block_mask, jnp.concatenate([wide] * PACK, axis=0), 0.0)
    mix_high[...], mix_low[...] = split(tall)


def prepare(parts, qmc_points):
    places = np.arange(HEAD)
    cosines = np.cos(np.pi * (places[:, None] + 0.5) * places[None, :] / HEAD)
    cosines = cosines * np.where(places == 0, math.sqrt(1.0 / HEAD), math.sqrt(2.0 / HEAD))[None, :]
    total = sum(item.shape[0] for item in parts)
    vectors, high, low = pl.pallas_call(
        prepare_kernel,
        out_shape=(
            jax.ShapeDtypeStruct((1, total), F32),
            jax.ShapeDtypeStruct((GROUP, GROUP), BF),
            jax.ShapeDtypeStruct((GROUP, GROUP), BF),
        ),
        compiler_params=params(),
        name="prepare",
    )(*parts, qmc_points, jnp.asarray(cosines * HEAD ** (-0.25), F32))
    return vectors, (high, low)


def stored(tile, info, own):
    return ((tile // own) ^ info[0]) * own + tile % own


def attention_front(info, normed, target, w_qkv, w_proj, vectors, mix, turns):
    total, dim = normed.shape
    half = dim // 2
    tiles = total // TILE
    front = lambda i, info: (stored(i, info, tiles // 2), 0)
    plain = lambda i, info: (i, 0)
    block = lambda k: pl.BlockSpec((dim, half), lambda i, info: (0, 2 * k + info[0]), pipeline_mode=pl.Buffered(1))
    groups = half // GROUP
    return pl.pallas_call(
        attn_front_kernel,
        out_shape=(
            *(jax.ShapeDtypeStruct((total, half), BF) for _ in range(8)),
            *(jax.ShapeDtypeStruct((1, half), F32) for _ in range(2)),
        ),
        grid_spec=pltpu.PrefetchScalarGridSpec(
            num_scalar_prefetch=1,
            grid=(tiles,),
            in_specs=[
                pl.BlockSpec((TILE, dim), front),
                pl.BlockSpec((TILE, dim), front),
                block(0),
                block(1),
                block(2),
                vector_spec(half, 5 * dim, 0),
                vector_spec(half, 6 * dim, 0),
                vector_spec(half, 7 * dim, 0),
                pl.BlockSpec((half, dim), lambda i, info: (info[0], 0), pipeline_mode=pl.Buffered(1)),
                vector_spec(half, 2 * dim, 0),
            ]
            + [whole(item.shape) for item in (*mix, *turns)],
            out_specs=[pl.BlockSpec((TILE, half), front)] * 2
            + [pl.BlockSpec((TILE, half), plain)] * 6
            + [whole((1, half))] * 2,
            scratch_shapes=[pltpu.VMEM((groups, GROUP, GROUP), F32), pltpu.VMEM((groups, 1, GROUP), F32)],
        ),
        compiler_params=params(),
        cost_estimate=cost(8 * total * dim * half + 64 * total * half * GROUP, 12 * total * dim, 2 * total * half),
        name="attention_front",
    )(info, normed, target, w_qkv, w_qkv, w_qkv, vectors, vectors, vectors, w_proj, vectors, *mix, *turns)


def attention_rear(info, saved, bias_q, scale_sum, w_qkv, vectors, shift, mix, turns):
    total, half = saved[0].shape
    dim = w_qkv.shape[0]
    tiles = total // TILE
    rear = lambda i, info: (stored(tiles - 1 - i, info, tiles // 2), 0)
    plain = lambda i, info: (tiles - 1 - i, 0)
    groups = half // GROUP
    return pl.pallas_call(
        partial(attn_rear_kernel, tiles),
        out_shape=(
            *(jax.ShapeDtypeStruct((total, half), BF) for _ in range(2)),
            jax.ShapeDtypeStruct((4, half), F32),
            jax.ShapeDtypeStruct((1, dim), F32),
        ),
        grid_spec=pltpu.PrefetchScalarGridSpec(
            num_scalar_prefetch=1,
            grid=(tiles,),
            in_specs=[pl.BlockSpec((TILE, half), plain)] * 6
            + [whole(item.shape) for item in (*mix, *turns, bias_q, scale_sum)]
            + [vector_spec(half, 2 * dim, 0), anywhere(), whole(shift.shape)],
            out_specs=[pl.BlockSpec((TILE, half), rear)] * 2 + [whole((4, half)), whole((1, dim))],
            scratch_shapes=[pltpu.VMEM((1, half), F32) for _ in range(3)]
            + [pltpu.VMEM((dim, 3 * half), BF), pltpu.SemaphoreType.DMA((3,))]
            + [pltpu.VMEM((groups, GROUP, GROUP), F32), pltpu.VMEM((groups, 1, GROUP), F32)],
        ),
        compiler_params=params(),
        cost_estimate=cost(48 * total * half * GROUP, 16 * total * half, 0),
        name="attention_rear",
    )(info, *saved, *mix, *turns, bias_q, scale_sum, vectors, w_qkv, shift)


def out_kernel(own, info, act, attended, w_proj, w_down, *rest):
    step = pl.program_id(0)
    if own:
        res, received, first, second, out, down_buf, sems = rest
    else:
        out, down_buf, sems = rest

    @pl.when(step == 0)
    def _():
        @pl.loop(0, down_buf.shape[0] // LANES)
        def _(j):
            strip_copy(info[0], w_down, down_buf, sems, 1, j).start()

        @pl.loop(0, down_buf.shape[0] // LANES)
        def _(j):
            strip_copy(info[0], w_down, down_buf, sems, 1, j).wait()

    value = mm(act[...], down_buf[...]) + mm(attended[...], w_proj[...])
    if own:
        value = value + received[...].astype(F32) + (first[...] + second[...]) + res[...].astype(F32)
    out[...] = value.astype(BF)


def out_rows(own, info, act, attended, w_proj, w_down, res=None, received=None, vectors=None):
    total, ff = act.shape
    dim = w_proj.shape[1]
    half = attended.shape[1]
    rows = total // 2
    tiles = rows // TILE
    shift = 0 if own else tiles
    shifted = lambda i, info: (i + shift, 0)
    plain = lambda i, info: (i, 0)
    extra, extra_specs = (), []
    if own:
        extra = (res, received, vectors, vectors)
        extra_specs = [pl.BlockSpec((TILE, dim), plain), pl.BlockSpec((TILE, dim), plain)]
        extra_specs += [vector_spec(dim, 3 * dim), vector_spec(dim, 4 * dim)]
    return pl.pallas_call(
        partial(out_kernel, own),
        out_shape=jax.ShapeDtypeStruct((rows, dim), BF),
        grid_spec=pltpu.PrefetchScalarGridSpec(
            num_scalar_prefetch=1,
            grid=(tiles,),
            in_specs=[
                pl.BlockSpec((TILE, ff), shifted),
                pl.BlockSpec((TILE, half), shifted),
                pl.BlockSpec((half, dim), lambda i, info: (info[0], 0), pipeline_mode=pl.Buffered(1)),
                anywhere(),
            ]
            + extra_specs,
            out_specs=pl.BlockSpec((TILE, dim), plain),
            scratch_shapes=[
                pltpu.VMEM((ff, dim), BF),
                pltpu.SemaphoreType.DMA((2, ff // LANES)),
            ],
        ),
        compiler_params=params(),
        cost_estimate=cost(2 * rows * dim * (ff + half), 2 * rows * (ff + half + dim) + 2 * dim * (ff + half)),
        name="out_rows",
    )(info, act, attended, w_proj, w_down, *extra)


def back_kernel(own, info, dq, dk, dv, up_grad, w_qkv, w_up, *rest):
    step = pl.program_id(0)
    if own:
        res, gain, target, received, out, w_buf, up_buf, part_sems, sems = rest
    else:
        out, w_buf, up_buf, part_sems, sems = rest
    grads = (dq, dk, dv)
    half = dq.shape[1]

    @pl.when(step == 0)
    def _():
        for p in range(3):
            part_copy(info[0], w_qkv, w_buf, part_sems, p).start()

        @pl.loop(0, up_buf.shape[1] // LANES)
        def _(j):
            strip_copy(info[0], w_up, up_buf, sems, 0, j).start()

        for p in range(3):
            part_copy(info[0], w_qkv, w_buf, part_sems, p).wait()

        @pl.loop(0, up_buf.shape[1] // LANES)
        def _(j):
            strip_copy(info[0], w_up, up_buf, sems, 0, j).wait()

    value = mm(up_grad[...], up_buf[...], NT)
    for p in range(3):
        value = value + mm(grads[p][...], w_buf[:, p * half : (p + 1) * half], NT)
    if own:
        xhat, rstd = norm_stats(res[...].astype(F32))
        scaled = (value + received[...].astype(F32)) * gain[...]
        middle = jnp.mean(scaled, axis=-1, keepdims=True)
        slope = jnp.mean(scaled * xhat, axis=-1, keepdims=True)
        out[...] = target[...].astype(F32) + rstd * (scaled - middle - xhat * slope)
    else:
        out[...] = value.astype(BF)


def back_rows(own, info, dq, dk, dv, up_grad, w_qkv, w_up, res=None, vectors=None, target=None, received=None):
    total, ff = up_grad.shape
    rows, dim = total // 2, w_qkv.shape[0]
    half = dq.shape[1]
    tiles = rows // TILE
    shift = 0 if own else tiles
    shifted = lambda i, info: (i + shift, 0)
    plain = lambda i, info: (i, 0)
    extra, extra_specs = (), []
    if own:
        extra = (res, vectors, target, received)
        extra_specs = [
            pl.BlockSpec((TILE, dim), plain),
            vector_spec(dim, 0),
            pl.BlockSpec((TILE, dim), plain),
            pl.BlockSpec((TILE, dim), plain),
        ]
    return pl.pallas_call(
        partial(back_kernel, own),
        out_shape=jax.ShapeDtypeStruct((rows, dim), F32 if own else BF),
        grid_spec=pltpu.PrefetchScalarGridSpec(
            num_scalar_prefetch=1,
            grid=(tiles,),
            in_specs=[pl.BlockSpec((TILE, half), shifted)] * 3
            + [pl.BlockSpec((TILE, ff), shifted), anywhere(), anywhere()]
            + extra_specs,
            out_specs=pl.BlockSpec((TILE, dim), plain),
            scratch_shapes=[
                pltpu.VMEM((dim, 3 * half), BF),
                pltpu.VMEM((dim, ff), BF),
                pltpu.SemaphoreType.DMA((3,)),
                pltpu.SemaphoreType.DMA((2, ff // LANES)),
            ],
        ),
        compiler_params=params(),
        cost_estimate=cost(2 * rows * dim * (ff + 3 * half), 2 * rows * (ff + 3 * half + 3 * dim) + 2 * dim * (ff + 3 * half)),
        name="back_rows",
    )(info, dq, dk, dv, up_grad, w_qkv, w_up, *extra)


def bit_orders(ndp):
    bits = [1 << j for j in range(ndp.bit_length() - 1)]
    return tuple(bits), tuple(bits[1::-1] + bits[2:])


def spots(me, ndp):
    apart = jnp.asarray(np.arange(ndp, dtype=np.int32)) ^ me
    rows = []
    for order in bit_orders(ndp):
        spot = jnp.zeros((ndp,), jnp.int32)
        for j, bit in enumerate(order):
            spot = spot + (((apart // bit) % 2) << (len(order) - 1 - j))
        rows.append(spot)
    return jnp.stack(rows)


def add(left, right, kind=BF):
    return (left.astype(F32) + right.astype(F32)).astype(kind)


def cross(value, bit, ndp):
    return lax.ppermute(value, "dp", [(i, i ^ bit) for i in range(ndp)])


class Reduction:
    def __init__(self, first, second, ndp):
        self.ndp = ndp
        self.orders = bit_orders(ndp)
        self.at = 0
        self.pairs = [first, second]
        self.fly()

    def fly(self):
        self.received = [
            cross(send, order[self.at], self.ndp) for (send, keep), order in zip(self.pairs, self.orders)
        ]

    def land(self, token=None):
        if token is not None:
            token, *self.received = lax.optimization_barrier((token, *self.received))
        self.step()
        return token

    def step(self):
        keeps = [keep for send, keep in self.pairs]
        self.at += 1
        steps = len(self.orders[0])
        if self.at == steps:
            parts = [add(k, r, F32)[0] for k, r in zip(keeps, self.received)]
            self.result = jnp.concatenate(parts, axis=0) if len(parts) > 1 else parts[0]
            return
        cut = keeps[0].shape[0] // 2
        pairs = [
            (add(k[cut:], r[cut:]), add(k[:cut], r[:cut])) for k, r in zip(keeps, self.received)
        ]
        if self.at == 2 and len(pairs) == 2:
            pairs = [tuple(jnp.concatenate(items, axis=1) for items in zip(*pairs))]
        self.pairs = pairs

    def hold(self, token):
        if self.at == len(self.orders[0]):
            token, self.result = lax.optimization_barrier((token, self.result))
        return token

    def finish(self):
        if 0 < self.at < len(self.orders[0]):
            self.fly()
        while self.at < len(self.orders[0]):
            self.land()
            if self.at < len(self.orders[0]):
                self.fly()
        return self.result

    def values(self):
        return [item for pair in self.pairs for item in pair]

    def after(self, token):
        if self.at < len(self.orders[0]):
            token, *items = lax.optimization_barrier((token, *self.values()))
            self.pairs = [(items[2 * j], items[2 * j + 1]) for j in range(len(items) // 2)]
            self.fly()
        else:
            token, self.result = lax.optimization_barrier((token, self.result))
        return token


def swap(value):
    return lax.ppermute(value, "stream", [(0, 1), (1, 0)])


def per_device(
    ndp, residual, cotangent, ln_gain, ln_bias, w_qkv, b_qkv, w_proj, b_proj, feature_scale,
    w_up, b_up, w_down, b_down, qmc_points, slot_lengths,
):
    own_rows, dim = residual.shape
    half = dim // 2
    ff = w_up.shape[1]
    side = lax.axis_index("stream")
    me = lax.axis_index("dp")
    info = jnp.stack([side, me, slot_lengths[0]]).astype(jnp.int32)
    table = spots(me, ndp)
    vectors, mix = prepare((ln_gain, ln_bias, feature_scale, b_proj, b_down, b_qkv, b_up), qmc_points)

    other_res = swap(residual)
    other_cot = swap(cotangent)
    *mine, target_sum = mlp_rows(0, info, residual, cotangent, vectors, w_up, w_down)
    normed, target, act, up_grad, upb, shift = mlp_rows(
        1, info, other_res, other_cot, vectors, w_up, w_down, mine
    )

    turns = tuple(jnp.asarray(item) for item in turn_tables())
    parts = mlp_weight_grads(ndp, table, act, target, normed, up_grad)
    mlp_sums = Reduction(parts[:2], parts[2:], ndp)

    attended, dq, *saved, bias_q, scale_sum = attention_front(
        info, normed, target, w_qkv, w_proj, vectors, mix, turns
    )
    attended = mlp_sums.land(attended)
    info = mlp_sums.after(info)
    dk, dv, sums, shift = attention_rear(info, saved, bias_q, scale_sum, w_qkv, vectors, shift, mix, turns)
    dk = mlp_sums.land(dk)
    table = mlp_sums.after(table)

    mine = lax.broadcasted_iota(jnp.int32, (1, 2, 1), 1) == side
    spread = lambda item: jnp.where(mine, item[:, None, :], 0.0)
    four = spread(sums)
    small = jnp.concatenate(
        [
            shift.reshape(ndp, -1),
            four[:3].reshape(ndp, -1),
            target_sum.reshape(ndp, -1),
            four[3].reshape(ndp, -1),
            spread(upb.reshape(-1, LANES)).reshape(ndp, -1),
        ],
        axis=1,
    )
    count = small.shape[1]
    extra = jnp.pad(small.astype(BF), ((0, 0), (0, 8 * half - count))).reshape(ndp, 8, half)
    parts = attn_weight_grads(ndp, table, normed, target, attended, dq, dk, dv, extra)
    attn_sums = Reduction(parts[:2], parts[2:], ndp)
    mlp_sums.land()
    info = mlp_sums.after(info)

    back_send = back_rows(False, info, dq, dk, dv, up_grad, w_qkv, w_up)
    back_send = attn_sums.land(back_send)
    info = attn_sums.after(info)
    back_received = swap(back_send)
    out_send = out_rows(False, info, act, attended, w_proj, w_down)
    out_send = attn_sums.land(mlp_sums.land(out_send))
    info = attn_sums.after(mlp_sums.after(info))
    out_received = swap(out_send)
    residual_grad = back_rows(
        True, info, dq, dk, dv, up_grad, w_qkv, w_up, residual, vectors, target, back_received
    )
    residual_grad = mlp_sums.hold(attn_sums.land(residual_grad))
    info = attn_sums.after(info)
    block_out = out_rows(True, info, act, attended, w_proj, w_down, residual, out_received, vectors)
    block_out = attn_sums.land(block_out)
    mlp_total, attn_total = mlp_sums.finish(), attn_sums.finish()

    blk = ff // (2 * ndp)
    size = dim // ndp
    small_size = size // 2
    down_rows = mlp_total[:blk]
    per = max(LANES // blk, 1)
    owners = [
        (v * 2 + s, (2 * (v // per) + s) * per + v % per) for v in range(ndp) for s in range(2)
    ]
    if any(a != b for a, b in owners):
        down_rows = lax.ppermute(down_rows, ("dp", "stream"), owners)

    def halves(blocks):
        blocks = blocks.reshape(blocks.shape[0], 2, small_size, blocks.shape[2])
        pick = lambda at: lax.dynamic_index_in_dim(blocks, at, 1, keepdims=False)
        return pick(side), pick(1 - side)

    def order(own, other):
        return jnp.where(side == 0, own, other), jnp.where(side == 0, other, own)

    keep, give = halves(mlp_total[blk:].reshape(2, size, -1))
    first, second = order(keep, swap(give))
    apart = lambda item: jnp.transpose(item, (1, 0, 2)).reshape(small_size, -1, 1, LANES)
    upw_grad = jnp.concatenate([apart(first), apart(second)], axis=2).reshape(small_size, ff)

    keep, give = halves(attn_total[: 3 * size].reshape(3, size, half))
    rest = attn_total[4 * size :]
    received = swap(jnp.concatenate([give.reshape(3 * small_size, half), rest], axis=0))
    first, second = order(keep, received[: 3 * small_size].reshape(3, small_size, half))
    qkvw_grad = jnp.concatenate([item[p] for p in range(3) for item in (first, second)], axis=1)
    proj_rows = jnp.concatenate(
        [attn_total[3 * size + p * small_size : 3 * size + (p + 1) * small_size] for p in range(2)], axis=1
    )
    proj_owners = [(v * 2 + s, ndp * s + v) for v in range(ndp) for s in range(2)]
    projw_grad = lax.ppermute(proj_rows, ("dp", "stream"), proj_owners)

    flat = (rest + received[3 * small_size :]).reshape(-1)
    ends = np.cumsum([0, size, 3 * size, size, size, 2 * blk])
    pieces = [
        lax.dynamic_index_in_dim(flat[a:b].reshape(2, -1), side, 0, keepdims=False)
        for a, b in zip(ends[:-1], ends[1:])
    ]
    shift_grad, qkvb_grad, projb_grad, scale_grad, upb_grad = pieces
    mine_at = (2 * me + side) * small_size
    near = lambda item: lax.dynamic_slice_in_dim(item, mine_at, small_size).astype(F32)
    along = jnp.sum(near(w_qkv) * qkvw_grad, axis=1) + jnp.sum(near(w_up) * upw_grad, axis=1)
    gain_grad = (along - near(ln_bias) * shift_grad) / near(ln_gain)

    return (
        block_out, residual_grad, gain_grad, shift_grad, qkvw_grad, qkvb_grad, projw_grad,
        projb_grad, scale_grad, upw_grad, upb_grad, down_rows, projb_grad,
    )


def solution(mesh):
    rows = P(("dp", "stream"), None)
    items = P(("dp", "stream"))
    return jax.shard_map(
        partial(per_device, mesh.shape["dp"]),
        mesh=mesh,
        in_specs=(rows, rows) + (P(),) * 12 + (P("dp"),),
        out_specs=(rows, rows, items, items, rows, items, rows, items, items, rows, items, rows, items),
        check_vma=False,
    )
```

profile of v0, /device:TPU:10, one launch (start us, length us, event | category | flops | bytes accessed | tf_op | source)
XLA Modules:
  0.0 268.6 jit_solution(17077210923199186734)
XLA Ops:
  0.7 0.5 collective-permute-start.1
  1.9 1.9 prepare.1
  3.7 0.6 pad_add_fusion.1.info
  4.3 0.6 pad_add_fusion.table
  4.9 21.8 %mlp_rows.2 = (bf16[2048,1024]{1,0:T(8,128)(2,1)}, bf16[2048,1024]{1,0:T(8,128)(2,1)}, bf16[2048,2048]{1,0:T(8,128)(2,1)}, bf16[2048,2048]{1,0:T(8,128)(2,1)}, f32[1,2048]{1,0:T(1,128)}, /*index=5*/f32[1,1024]{1,0:T(1,128)}) custom-call(s32[3]{0:T(128)} %pad_add_fusion.1.info, bf16[1024,1024]{1,0:T(8,128)(2,1)} %rest_0_.3, bf16[1024,1024]{1,0:T(8,128)(2,1)} %cot.1, ...), custom_call_target="tpu_custom_call" | custom-call | flops 3435973888 | bytes 18454936 | tf_op jit(solution)/shard_map/mlp_rows/pallas_call | solution.py:187
  26.7 23.8 %mlp_rows.3 = (bf16[2048,1024]{1,0:T(8,128)(2,1)}, bf16[2048,1024]{1,0:T(8,128)(2,1)}, bf16[2048,2048]{1,0:T(8,128)(2,1)}, bf16[2048,2048]{1,0:T(8,128)(2,1)}, f32[1,2048]{1,0:T(1,128)}, /*index=5*/f32[1,1024]{1,0:T(1,128)}) custom-call(s32[3]{0:T(128)} %pad_add_fusion.1.info, ...), custom_call_target="tpu_custom_call", output_to_operand_aliasing={{0}: (8, {}), {1}: (9, {}), {2}: (10, {}), {3}: (11, {})} | custom-call | flops 3435973888 | bytes 18454936 | tf_op jit(solution)/shard_map/mlp_rows/pallas_call | solution.py:187
  50.6 24.6 %mlp_weight_grads.1 = (bf16[8,128,1024]{2,1,0:T(8,128)(2,1)}, bf16[8,128,1024]{2,1,0:T(8,128)(2,1)}, bf16[8,128,1024]{2,1,0:T(8,128)(2,1)}, bf16[8,128,1024]{2,1,0:T(8,128)(2,1)}) custom-call(s32[2,16]{1,0:T(2,128)} %pad_add_fusion.table, bf16[2048,2048]{1,0:T(8,128)(2,1)} %get-tuple-element.100.act, bf16[2048,1024]{1,0:T(8,128)(2,1)} %get-tuple-element.101.target.rest_2_, ...), custom_call_target="tpu_custom_call" | custom-call | flops 6871947776 | bytes 13421772 | tf_op jit(solution)/shard_map/mlp_weight_grads/pallas_call | solution.py:295
  75.2 0.6 collective-permute-start.2
  75.8 1.5 collective-permute-start.3
  77.3 42.6 %attention_front.1 = (bf16[2048,512]{1,0:T(8,128)(2,1)}, bf16[2048,512]{1,0:T(8,128)(2,1)}, bf16[2048,512]{1,0:T(8,128)(2,1)}, bf16[2048,512]{1,0:T(8,128)(2,1)}...) custom-call(s32[3]{0:T(128)} %pad_add_fusion.1.info, ...), custom_call_target="tpu_custom_call" | custom-call | flops 10307921920 | bytes 10066329 | tf_op jit(solution)/shard_map/attention_front/pallas_call | solution.py:664
  119.9 3.2 %collective-permute-done.2 = bf16[8,128,1024]{2,1,0:T(8,128)(2,1)S(1)} collective-permute-done((bf16[8,128,1024]{2,1,0:T(8,128)(2,1)}, bf16[8,128,1024]{2,1,0:T(8,128)(2,1)S(1)}, u32[]{:S(2)}, u32[]{:S(2)}) %collective-permute-start.2) | collective-permute-done | bytes 2097184 | tf_op jit(solution)/shard_map/ppermute | solution.py:889
  123.1 0.2 collective-permute-done.3
  123.3 1.9 add_convert_fusion
  125.2 2.0 add_convert_fusion.2
  127.2 1.5 collective-permute-start.4
  128.7 1.5 collective-permute-start.5
  130.5 21.5 %attention_rear.1 = (bf16[2048,512]{1,0:T(8,128)(2,1)}, bf16[2048,512]{1,0:T(8,128)(2,1)}, f32[4,512]{1,0:T(4,128)}, f32[1,1024]{1,0:T(1,128)}) custom-call(s32[3]{0:T(128)} %pad_add_fusion.1.info, bf16[2048,512]{1,0:T(8,128)(2,1)} %get-tuple-element.115.fq_s, bf16[2048,512]{1,0:T(8,128)(2,1)} %get-tuple-element.116.fk_s, ...), custom_call_target="tpu_custom_call" | custom-call | flops 5153960960 | bytes 6710886 | tf_op jit(solution)/shard_map/attention_rear/pallas_call | solution.py:704
  152.0 0.8 collective-permute-done.5
  152.8 1.6 add_convert_fusion.11
  154.3 0.4 add_convert_fusion.10
  154.9 0.5 collective-permute-start.6
  155.8 0.1 concatenate.30
  155.9 0.7 copy.55
  156.6 16.8 %attn_weight_grads.1 = (bf16[8,128,512]{2,1,0:T(8,128)(2,1)}, bf16[8,128,512]{2,1,0:T(8,128)(2,1)}, bf16[8,136,512]{2,1,0:T(8,128)(2,1)}, bf16[8,136,512]{2,1,0:T(8,128)(2,1)}) custom-call(s32[2,16]{1,0:T(2,128)} %pad_add_fusion.table, bf16[2048,1024]{1,0:T(8,128)(2,1)} %get-tuple-element.102.normed, bf16[2048,512]{1,0:T(8,128)(2,1)} %get-tuple-element.134.attended, ...), custom_call_target="tpu_custom_call" | custom-call | flops 3435973888 | bytes 8388608 | tf_op jit(solution)/shard_map/attn_weight_grads/pallas_call | solution.py:359
  173.5 0.7 collective-permute-start.8
  174.2 1.4 collective-permute-start.7
  175.5 2.5 collective-permute-done.6
  178.0 0.4 add_convert_fusion.8
  178.4 2.6 collective-permute-start.9
  181.0 15.0 %back_rows.2 = bf16[1024,1024]{1,0:T(8,128)(2,1)} custom-call(s32[3]{0:T(128)} %pad_add_fusion.1.info, bf16[2048,512]{1,0:T(8,128)(2,1)} %get-tuple-element.135.dq, bf16[2048,512]{1,0:T(8,128)(2,1)} %get-tuple-element.136.dk, bf16[2048,512]{1,0:T(8,128)(2,1)} %get-tuple-element.137.dv, bf16[2048,2048]{1,0:T(8,128)(2,1)} %get-tuple-element.103.up_grad, ...), custom_call_target="tpu_custom_call" | custom-call | flops 3006477056 | bytes 8388608 | tf_op jit(solution)/shard_map/back_rows/pallas_call | solution.py:845
  196.0 1.0 collective-permute-done.7
  197.0 1.1 collective-permute-done.8
  198.2 0.3 add_convert_fusion.4
  198.5 0.3 add_convert_fusion.6
  198.8 1.4 collective-permute-start.11
  200.2 0.5 collective-permute-start.10
  200.8 11.8 %out_rows.2 = bf16[1024,1024]{1,0:T(8,128)(2,1)} custom-call(s32[3]{0:T(128)} %pad_add_fusion.1.info, bf16[2048,2048]{1,0:T(8,128)(2,1)} %get-tuple-element.100.act, bf16[2048,512]{1,0:T(8,128)(2,1)} %get-tuple-element.134.attended, bf16[1024,1024]{1,0:T(8,128)(2,1)} %w_proj.5, bf16[4096,1024]{1,0:T(8,128)(2,1)} %w_down.7), custom_call_target="tpu_custom_call" | custom-call | flops 2147483648 | bytes 5033164 | tf_op jit(solution)/shard_map/out_rows/pallas_call | solution.py:765
  212.6 0.2 add_bitcast_fusion
  212.8 1.5 collective-permute-done.10
  214.3 0.1 add_convert_fusion.18
  214.4 0.1 add_convert_fusion.14
  214.7 1.4 collective-permute-start.13
  216.0 17.4 %back_rows.3 = f32[1024,1024]{1,0:T(8,128)} custom-call(s32[3]{0:T(128)} %pad_add_fusion.1.info, bf16[2048,512]{1,0:T(8,128)(2,1)} %get-tuple-element.135.dq, bf16[2048,512]{1,0:T(8,128)(2,1)} %get-tuple-element.136.dk, bf16[2048,512]{1,0:T(8,128)(2,1)} %get-tuple-element.137.dv, bf16[2048,2048]{1,0:T(8,128)(2,1)} %get-tuple-element.103.up_grad, ...), custom_call_target="tpu_custom_call" | custom-call | flops 3006477056 | bytes 8388608 | tf_op jit(solution)/shard_map/back_rows/pallas_call | solution.py:845
  233.5 0.9 fusion.21
  234.4 0.3 collective-permute-start.17
  234.7 0.1 add_convert_fusion.16
  234.8 2.6 collective-permute-start.15
  237.5 0.2 copy.48
  237.7 0.2 reshape.96
  237.9 0.2 copy.49
  238.1 0.2 reshape.97
  238.4 0.4 copy.50
  238.8 0.4 reshape.98
  239.2 12.7 %out_rows.3 = bf16[1024,1024]{1,0:T(8,128)(2,1)} custom-call(s32[3]{0:T(128)} %pad_add_fusion.1.info, bf16[2048,2048]{1,0:T(8,128)(2,1)} %get-tuple-element.100.act, bf16[2048,512]{1,0:T(8,128)(2,1)} %get-tuple-element.134.attended, bf16[1024,1024]{1,0:T(8,128)(2,1)} %w_proj.5, bf16[4096,1024]{1,0:T(8,128)(2,1)} %w_down.7, bf16[1024,1024]{1,0:T(8,128)(2,1)} %rest_0_.3, ...), custom_call_target="tpu_custom_call" | custom-call | flops 2147483648 | bytes 5033164 | tf_op jit(solution)/shard_map/out_rows/pallas_call | solution.py:765
  252.3 3.1 %collective-permute-start.18 = (f32[32,1024]{1,0:T(8,128)S(1)}, f32[32,1024]{1,0:T(8,128)S(1)}, u32[]{:S(2)}, u32[]{:S(2)}) collective-permute-start(f32[32,1024]{1,0:T(8,128)S(1)} %pad_maximum_fusion.6), channel_id=1, source_target_pairs={{0,0},{1,16},{2,1},{3,17},{4,2},{5,18},{6,3},{7,19},{8,4},{9,20},{... | collective-permute-start | bytes 393224 | tf_op jit(solution)/shard_map/ppermute | solution.py:1061
  255.4 1.1 multiply_reduce_fusion
  256.5 6.3 %collective-permute-done.18 = f32[32,1024]{1,0:T(8,128)S(1)} collective-permute-done((f32[32,1024]{1,0:T(8,128)S(1)}, f32[32,1024]{1,0:T(8,128)S(1)}, u32[]{:S(2)}, u32[]{:S(2)}) %collective-permute-start.18) | collective-permute-done | bytes 131104 | tf_op jit(solution)/shard_map/ppermute | solution.py:1061
  263.0 0.5 fusion.17
  263.7 1.2 multiply_reduce_fusion.1
  265.1 0.5 fusion.15
  265.6 0.5 fusion.18
  266.1 1.3 convert_divide_fusion
  267.4 0.5 copy.70
  267.9 0.7 copy.71
  (83 shorter events, 1.7 us)
Async XLA Ops:
  0.6 26.1 %collective-permute-start = (bf16[1024,1024]{1,0:T(8,128)(2,1)}, bf16[1024,1024]{1,0:T(8,128)(2,1)}, u32[]{:S(2)}, u32[]{:S(2)}) collective-permute-start(bf16[1024,1024]{1,0:T(8,128)(2,1)} %rest_0_.3), channel_id=1, source_target_pairs={{0,1},{1,0},{2,3},{3,2},{4,5},{5,4},{6,7},{7,6},{8,9},{9,8},{10,11... | collective-permute-start | bytes 6291464 | tf_op jit(solution)/shard_map/ppermute | solution.py:955
  0.7 26.0 %collective-permute-start.1 = (bf16[1024,1024]{1,0:T(8,128)(2,1)}, bf16[1024,1024]{1,0:T(8,128)(2,1)}, u32[]{:S(2)}, u32[]{:S(2)}) collective-permute-start(bf16[1024,1024]{1,0:T(8,128)(2,1)} %cot.1), channel_id=1, source_target_pairs={{0,1},{1,0},{2,3},{3,2},{4,5},{5,4},{6,7},{7,6},{8,9},{9,8},{10,11... | collective-permute-start | bytes 6291464 | tf_op jit(solution)/shard_map/ppermute | solution.py:955
  75.2 47.9 %collective-permute-start.2 = (bf16[8,128,1024]{2,1,0:T(8,128)(2,1)}, bf16[8,128,1024]{2,1,0:T(8,128)(2,1)S(1)}, u32[]{:S(2)}, u32[]{:S(2)}) collective-permute-start(bf16[8,128,1024]{2,1,0:T(8,128)(2,1)} %get-tuple-element.108), channel_id=1, source_target_pairs={{0,2},{2,0},{4,6},{6,4},{8,10},{10,8},{12,14},{14,12},{16,18},{18,... | collective-permute-start | bytes 6291464 | tf_op jit(solution)/shard_map/ppermute | solution.py:889
  75.8 47.5 %collective-permute-start.3 = (bf16[8,128,1024]{2,1,0:T(8,128)(2,1)}, bf16[8,128,1024]{2,1,0:T(8,128)(2,1)S(1)}, u32[]{:S(2)}, u32[]{:S(2)}) collective-permute-start(bf16[8,128,1024]{2,1,0:T(8,128)(2,1)} %get-tuple-element.109), channel_id=1, source_target_pairs={{0,4},{2,6},{4,0},{6,2},{8,12},{10,14},{12,8},{14,10},{16,20},{18,... | collective-permute-start | bytes 6291464 | tf_op jit(solution)/shard_map/ppermute | solution.py:889
  77.3 46.0 %copy-start.1 = (bf16[8,128,1024]{2,1,0:T(8,128)(2,1)S(1)}, bf16[8,128,1024]{2,1,0:T(8,128)(2,1)}, u32[]{:S(2)}) copy-start(bf16[8,128,1024]{2,1,0:T(8,128)(2,1)} %get-tuple-element.111) | copy-start | bytes 6291460
  123.3 1.9 copy-start
  125.2 5.0 %copy-start.8 = (f32[1,1024]{1,0:T(1,128)S(1)}, f32[1,1024]{1,0:T(1,128)}, u32[]{:S(2)}) copy-start(f32[1,1024]{1,0:T(1,128)} %get-tuple-element.140) | copy-start | bytes 12292
  125.2 5.2 %copy-start.6 = (f32[1,2048]{1,0:T(1,128)S(1)}, f32[1,2048]{1,0:T(1,128)}, u32[]{:S(2)}) copy-start(f32[1,2048]{1,0:T(1,128)} %get-tuple-element.141) | copy-start | bytes 24580
  127.2 24.8 %collective-permute-start.4 = (bf16[4,128,1024]{2,1,0:T(8,128)(2,1)}, bf16[4,128,1024]{2,1,0:T(8,128)(2,1)}, u32[]{:S(2)}, u32[]{:S(2)}) collective-permute-start(bf16[4,128,1024]{2,1,0:T(8,128)(2,1)} %get-tuple-element.125), channel_id=1, source_target_pairs={{0,4},{2,6},{4,0},{6,2},{8,12},{10,14},{12,8},{14,10},{16,20},{18,... | collective-permute-start | bytes 3145736 | tf_op jit(solution)/shard_map/ppermute | solution.py:889
  128.7 24.0 %collective-permute-start.5 = (bf16[4,128,1024]{2,1,0:T(8,128)(2,1)}, bf16[4,128,1024]{2,1,0:T(8,128)(2,1)S(1)}, u32[]{:S(2)}, u32[]{:S(2)}) collective-permute-start(bf16[4,128,1024]{2,1,0:T(8,128)(2,1)} %get-tuple-element.126), channel_id=1, source_target_pairs={{0,2},{2,0},{4,6},{6,4},{8,10},{10,8},{12,14},{14,12},{16,18},{18,... | collective-permute-start | bytes 3145736 | tf_op jit(solution)/shard_map/ppermute | solution.py:889
  154.7 0.7 copy-start.7
  154.8 1.0 copy-start.9
  154.9 23.1 %collective-permute-start.6 = (bf16[2,256,1024]{2,1,0:T(8,128)(2,1)S(1)}, bf16[2,256,1024]{2,1,0:T(8,128)(2,1)S(1)}, u32[]{:S(2)}, u32[]{:S(2)}) collective-permute-start(bf16[2,256,1024]{2,1,0:T(8,128)(2,1)S(1)} %pad_maximum_fusion), channel_id=1, source_target_pairs={{0,8},{2,10},{4,12},{6,14},{8,0},{10,2},{12,4},{14,6},{16,24},{18,... | collective-permute-start | bytes 3145736 | tf_op jit(solution)/shard_map/ppermute | solution.py:889
  173.5 24.7 %collective-permute-start.8 = (bf16[8,136,512]{2,1,0:T(8,128)(2,1)}, bf16[8,136,512]{2,1,0:T(8,128)(2,1)S(1)}, u32[]{:S(2)}, u32[]{:S(2)}) collective-permute-start(bf16[8,136,512]{2,1,0:T(8,128)(2,1)} %get-tuple-element.144), channel_id=1, source_target_pairs={{0,4},{2,6},{4,0},{6,2},{8,12},{10,14},{12,8},{14,10},{16,20},{18,... | collective-permute-start | bytes 3342344 | tf_op jit(solution)/shard_map/ppermute | solution.py:889
  174.2 22.9 %collective-permute-start.7 = (bf16[8,128,512]{2,1,0:T(8,128)(2,1)}, bf16[8,128,512]{2,1,0:T(8,128)(2,1)S(1)}, u32[]{:S(2)}, u32[]{:S(2)}) collective-permute-start(bf16[8,128,512]{2,1,0:T(8,128)(2,1)} %get-tuple-element.143), channel_id=1, source_target_pairs={{0,2},{2,0},{4,6},{6,4},{8,10},{10,8},{12,14},{14,12},{16,18},{18,... | collective-permute-start | bytes 3145736 | tf_op jit(solution)/shard_map/ppermute | solution.py:889
  178.4 19.8 %copy-start.3 = (bf16[8,136,512]{2,1,0:T(8,128)(2,1)S(1)}, bf16[8,136,512]{2,1,0:T(8,128)(2,1)}, u32[]{:S(2)}) copy-start(bf16[8,136,512]{2,1,0:T(8,128)(2,1)} %get-tuple-element.146) | copy-start | bytes 3342340
  178.4 34.2 %collective-permute-start.9 = (bf16[1,256,1024]{2,1,0:T(8,128)(2,1)S(1)}, bf16[1,256,1024]{2,1,0:T(8,128)(2,1)S(1)}, u32[]{:S(2)}, u32[]{:S(2)}) collective-permute-start(bf16[1,256,1024]{2,1,0:T(8,128)(2,1)S(1)} %get-tuple-element.150), channel_id=1, source_target_pairs={{0,16},{2,18},{4,20},{6,22},{8,24},{10,26},{12,28},{14,30},{16,0},... | collective-permute-start | bytes 1572872 | tf_op jit(solution)/shard_map/ppermute | solution.py:889
  196.0 2.5 copy-start.4
  198.2 17.9 %collective-permute-start.12 = (bf16[1024,1024]{1,0:T(8,128)(2,1)}, bf16[1024,1024]{1,0:T(8,128)(2,1)}, u32[]{:S(2)}, u32[]{:S(2)}) collective-permute-start(bf16[1024,1024]{1,0:T(8,128)(2,1)} %back_rows.2), channel_id=1, source_target_pairs={{0,1},{1,0},{2,3},{3,2},{4,5},{5,4},{6,7},{7,6},{8,9},{9,8},{10,11... | collective-permute-start | bytes 6291464 | tf_op jit(solution)/shard_map/ppermute | solution.py:955
  198.8 15.5 %collective-permute-start.11 = (bf16[4,136,512]{2,1,0:T(8,128)(2,1)S(1)}, bf16[4,136,512]{2,1,0:T(8,128)(2,1)S(1)}, u32[]{:S(2)}, u32[]{:S(2)}) collective-permute-start(bf16[4,136,512]{2,1,0:T(8,128)(2,1)S(1)} %get-tuple-element.156), channel_id=1, source_target_pairs={{0,2},{2,0},{4,6},{6,4},{8,10},{10,8},{12,14},{14,12},{16,18},{18,... | collective-permute-start | bytes 1671176 | tf_op jit(solution)/shard_map/ppermute | solution.py:889
  200.2 14.1 %collective-permute-start.10 = (bf16[4,128,512]{2,1,0:T(8,128)(2,1)S(1)}, bf16[4,128,512]{2,1,0:T(8,128)(2,1)S(1)}, u32[]{:S(2)}, u32[]{:S(2)}) collective-permute-start(bf16[4,128,512]{2,1,0:T(8,128)(2,1)S(1)} %get-tuple-element.155), channel_id=1, source_target_pairs={{0,4},{2,6},{4,0},{6,2},{8,12},{10,14},{12,8},{14,10},{16,20},{18,... | collective-permute-start | bytes 1572872 | tf_op jit(solution)/shard_map/ppermute | solution.py:889
  214.3 25.0 %collective-permute-start.14 = (bf16[1024,1024]{1,0:T(8,128)(2,1)}, bf16[1024,1024]{1,0:T(8,128)(2,1)}, u32[]{:S(2)}, u32[]{:S(2)}) collective-permute-start(bf16[1024,1024]{1,0:T(8,128)(2,1)} %out_rows.2), channel_id=1, source_target_pairs={{0,1},{1,0},{2,3},{3,2},{4,5},{5,4},{6,7},{7,6},{8,9},{9,8},{10,11... | collective-permute-start | bytes 6291464 | tf_op jit(solution)/shard_map/ppermute | solution.py:955
  214.7 18.8 %collective-permute-start.13 = (bf16[2,264,512]{2,1,0:T(8,128)(2,1)S(1)}, bf16[2,264,512]{2,1,0:T(8,128)(2,1)S(1)}, u32[]{:S(2)}, u32[]{:S(2)}) collective-permute-start(bf16[2,264,512]{2,1,0:T(8,128)(2,1)S(1)} %pad_maximum_fusion.2), channel_id=1, source_target_pairs={{0,8},{2,10},{4,12},{6,14},{8,0},{10,2},{12,4},{14,6},{16,24},{18,... | collective-permute-start | bytes 1622024 | tf_op jit(solution)/shard_map/ppermute | solution.py:889
  234.4 3.0 %collective-permute-start.17 = (f32[2,32,1024]{2,1,0:T(8,128)S(1)}, f32[2,32,1024]{2,1,0:T(8,128)S(1)}, u32[]{:S(2)}, u32[]{:S(2)}) collective-permute-start(f32[2,32,1024]{2,1,0:T(8,128)S(1)} %dynamic-slice_bitcast_fusion), channel_id=1, source_target_pairs={{0,1},{1,0},{2,3},{3,2},{4,5},{5,4},{6,7},{7,6},{8,9},{9,8},{10,11... | collective-permute-start | bytes 786440 | tf_op jit(solution)/shard_map/ppermute | solution.py:955
  234.8 17.1 %collective-permute-start.15 = (bf16[1,264,512]{2,1,0:T(8,128)(2,1)S(1)}, bf16[1,264,512]{2,1,0:T(8,128)(2,1)S(1)}, u32[]{:S(2)}, u32[]{:S(2)}) collective-permute-start(bf16[1,264,512]{2,1,0:T(8,128)(2,1)S(1)} %get-tuple-element.167), channel_id=1, source_target_pairs={{0,16},{2,18},{4,20},{6,22},{8,24},{10,26},{12,28},{14,30},{16,0},... | collective-permute-start | bytes 811016 | tf_op jit(solution)/shard_map/ppermute | solution.py:889
  239.2 16.2 %copy-start.2 = (f32[32,4096]{1,0:T(8,128)}, f32[32,4096]{1,0:T(8,128)S(1)}, u32[]{:S(2)}) copy-start(f32[32,4096]{1,0:T(8,128)S(1)} %reshape.98) | copy-start | bytes 1572868
  252.2 10.7 %collective-permute-start.16 = (f32[104,512]{1,0:T(8,128)S(1)}, f32[104,512]{1,0:T(8,128)S(1)}, u32[]{:S(2)}, u32[]{:S(2)}) collective-permute-start(f32[104,512]{1,0:T(8,128)S(1)} %pad_maximum_fusion.5), channel_id=1, source_target_pairs={{0,1},{1,0},{2,3},{3,2},{4,5},{5,4},{6,7},{7,6},{8,9},{9,8},{10,11... | collective-permute-start | bytes 638984 | tf_op jit(solution)/shard_map/ppermute | solution.py:955
  252.3 10.6 %collective-permute-start.18 = (f32[32,1024]{1,0:T(8,128)S(1)}, f32[32,1024]{1,0:T(8,128)S(1)}, u32[]{:S(2)}, u32[]{:S(2)}) collective-permute-start(f32[32,1024]{1,0:T(8,128)S(1)} %pad_maximum_fusion.6), channel_id=1, source_target_pairs={{0,0},{1,16},{2,1},{3,17},{4,2},{5,18},{6,3},{7,19},{8,4},{9,20},{... | collective-permute-start | bytes 393224 | tf_op jit(solution)/shard_map/ppermute | solution.py:1061
  263.0 5.6 %copy-start.10 = (f32[32]{0:T(128)}, f32[32]{0:T(128)S(1)}, u32[]{:S(2)}) copy-start(f32[32]{0:T(128)S(1)} %fusion.16) | copy-start | bytes 388
  263.7 4.9 %copy-start.5 = (f32[32,3072]{1,0:T(8,128)}, f32[32,3072]{1,0:T(8,128)S(1)}, u32[]{:S(2)}) copy-start(f32[32,3072]{1,0:T(8,128)S(1)} %fusion.2) | copy-start | bytes 1179652
where the time goes:
time: 269 us
  Pallas kernels  210 us (78%)
  starting transfers between devices  20.2 us (8%)
  waiting for transfers between devices  16.7 us (6%)
  other arithmetic  12.9 us (5%)
  local copies, waits for them, and re-layouts  6.97 us (3%)
    pallas_call x2, Pallas kernels, mlp_rows(): pl.pallas_call(partial(mlp_kernel, half, tiles), out_shape=outs, grid_spe...  45.6 us
    pallas_call x1, Pallas kernels, attention_front(): pl.pallas_call(attn_front_kernel, out_shape=(*(jax.ShapeDtypeStruct((tota...  42.6 us
    pallas_call x2, Pallas kernels, back_rows(): pl.pallas_call(partial(back_kernel, own), out_shape=jax.ShapeDtypeStruct(...  32.5 us
    pallas_call x1, Pallas kernels, mlp_weight_grads(): pl.pallas_call(partial(mlp_grad_kernel, tiles), out_shape=(shape,) * 4, g...  24.6 us
    pallas_call x2, Pallas kernels, out_rows(): pl.pallas_call(partial(out_kernel, own), out_shape=jax.ShapeDtypeStruct((...  24.5 us
    pallas_call x1, Pallas kernels, attention_rear(): pl.pallas_call(partial(attn_rear_kernel, tiles), out_shape=(*(jax.ShapeDt...  21.5 us
    pallas_call x1, Pallas kernels, attn_weight_grads(): pl.pallas_call(attn_grad_kernel, out_shape=(shapes[0], shapes[0], shapes[...  16.8 us
    ppermute x12, starting transfers between devices, cross(): return lax.ppermute(value, 'dp', [(i, i ^ bit) for i in range(ndp)])  16.2 us
  transfers between devices with their start and end apart: 19, of which 8 were waited for; matrix products, arithmetic and copies ran while one was open for 3% of the time, Pallas kernels for 60%

commit v1 on v0

--- a/solution.py
+++ b/solution.py
@@ -162,9 +162,9 @@
         def _():
             sums[...] = jnp.zeros_like(sums)
 
-            @pl.loop(0, upb.shape[1] // GROUP)
+            @pl.loop(0, upb.shape[1] // (2 * GROUP))
             def _(j):
-                cols = pl.ds(pl.multiple_of(j * GROUP, GROUP), GROUP)
+                cols = pl.ds(pl.multiple_of(j * 2 * GROUP, GROUP), 2 * GROUP)
                 sums[...] += exact_row(upb[:, cols], up_buf[:, cols])
 
 

time: 269 us -> 269 us (level)
  no operation moved by 1% of the time
where the time goes in v1:
time: 269 us; the launch traced here: 268 us
  Pallas kernels  209 us (78%)
  starting transfers between devices  20.2 us (8%)
  waiting for transfers between devices  16.7 us (6%)
  other arithmetic  12.9 us (5%)
  local copies, waits for them, and re-layouts  6.97 us (3%)
    pallas_call x2, Pallas kernels, mlp_rows(): pl.pallas_call(partial(mlp_kernel, half, tiles), out_shape=outs, grid_spe...  45.1 us
    pallas_call x1, Pallas kernels, attention_front(): pl.pallas_call(attn_front_kernel, out_shape=(*(jax.ShapeDtypeStruct((tota...  42.6 us
    pallas_call x2, Pallas kernels, back_rows(): pl.pallas_call(partial(back_kernel, own), out_shape=jax.ShapeDtypeStruct(...  32.5 us
    pallas_call x1, Pallas kernels, mlp_weight_grads(): pl.pallas_call(partial(mlp_grad_kernel, tiles), out_shape=(shape,) * 4, g...  24.6 us
    pallas_call x2, Pallas kernels, out_rows(): pl.pallas_call(partial(out_kernel, own), out_shape=jax.ShapeDtypeStruct((...  24.5 us
    pallas_call x1, Pallas kernels, attention_rear(): pl.pallas_call(partial(attn_rear_kernel, tiles), out_shape=(*(jax.ShapeDt...  21.5 us
    pallas_call x1, Pallas kernels, attn_weight_grads(): pl.pallas_call(attn_grad_kernel, out_shape=(shapes[0], shapes[0], shapes[...  16.8 us
    ppermute x12, starting transfers between devices, cross(): return lax.ppermute(value, 'dp', [(i, i ^ bit) for i in range(ndp)])  16.2 us
  transfers between devices with their start and end apart: 19, of which 8 were waited for; matrix products, arithmetic and copies ran while one was open for 3% of the time, Pallas kernels for 60%

profile of v1, /device:TPU:10, one launch (start us, length us, event | category | flops | bytes accessed | tf_op | source)
XLA Modules:
  0.0 268.1 jit_solution(6820487637356173387)
XLA Ops:
  0.7 0.5 collective-permute-start.1
  1.9 1.9 prepare.1
  3.7 0.6 pad_add_fusion.1.info
  4.3 0.6 pad_add_fusion.table
  4.9 21.8 %mlp_rows.2 = (bf16[2048,1024]{1,0:T(8,128)(2,1)}, bf16[2048,1024]{1,0:T(8,128)(2,1)}, bf16[2048,2048]{1,0:T(8,128)(2,1)}, bf16[2048,2048]{1,0:T(8,128)(2,1)}, f32[1,2048]{1,0:T(1,128)}, /*index=5*/f32[1,1024]{1,0:T(1,128)}) custom-call(s32[3]{0:T(128)} %pad_add_fusion.1.info, bf16[1024,1024]{1,0:T(8,128)(2,1)} %rest_0_.3, bf16[1024,1024]{1,0:T(8,128)(2,1)} %cot.1, ...), custom_call_target="tpu_custom_call" | custom-call | flops 3435973888 | bytes 18454936 | tf_op jit(solution)/shard_map/mlp_rows/pallas_call | solution.py:187
  26.7 23.3 %mlp_rows.3 = (bf16[2048,1024]{1,0:T(8,128)(2,1)}, bf16[2048,1024]{1,0:T(8,128)(2,1)}, bf16[2048,2048]{1,0:T(8,128)(2,1)}, bf16[2048,2048]{1,0:T(8,128)(2,1)}, f32[1,2048]{1,0:T(1,128)}, /*index=5*/f32[1,1024]{1,0:T(1,128)}) custom-call(s32[3]{0:T(128)} %pad_add_fusion.1.info, ...), custom_call_target="tpu_custom_call", output_to_operand_aliasing={{0}: (8, {}), {1}: (9, {}), {2}: (10, {}), {3}: (11, {})} | custom-call | flops 3435973888 | bytes 18454936 | tf_op jit(solution)/shard_map/mlp_rows/pallas_call | solution.py:187
  50.0 24.6 %mlp_weight_grads.1 = (bf16[8,128,1024]{2,1,0:T(8,128)(2,1)}, bf16[8,128,1024]{2,1,0:T(8,128)(2,1)}, bf16[8,128,1024]{2,1,0:T(8,128)(2,1)}, bf16[8,128,1024]{2,1,0:T(8,128)(2,1)}) custom-call(s32[2,16]{1,0:T(2,128)} %pad_add_fusion.table, bf16[2048,2048]{1,0:T(8,128)(2,1)} %get-tuple-element.100.act, bf16[2048,1024]{1,0:T(8,128)(2,1)} %get-tuple-element.101.target.rest_2_, ...), custom_call_target="tpu_custom_call" | custom-call | flops 6871947776 | bytes 13421772 | tf_op jit(solution)/shard_map/mlp_weight_grads/pallas_call | solution.py:295
  74.7 0.6 collective-permute-start.2
  75.3 1.5 collective-permute-start.3
  76.8 42.6 %attention_front.1 = (bf16[2048,512]{1,0:T(8,128)(2,1)}, bf16[2048,512]{1,0:T(8,128)(2,1)}, bf16[2048,512]{1,0:T(8,128)(2,1)}, bf16[2048,512]{1,0:T(8,128)(2,1)}...) custom-call(s32[3]{0:T(128)} %pad_add_fusion.1.info, ...), custom_call_target="tpu_custom_call" | custom-call | flops 10307921920 | bytes 10066329 | tf_op jit(solution)/shard_map/attention_front/pallas_call | solution.py:664
  119.4 3.2 %collective-permute-done.2 = bf16[8,128,1024]{2,1,0:T(8,128)(2,1)S(1)} collective-permute-done((bf16[8,128,1024]{2,1,0:T(8,128)(2,1)}, bf16[8,128,1024]{2,1,0:T(8,128)(2,1)S(1)}, u32[]{:S(2)}, u32[]{:S(2)}) %collective-permute-start.2) | collective-permute-done | bytes 2097184 | tf_op jit(solution)/shard_map/ppermute | solution.py:889
  122.6 0.2 collective-permute-done.3
  122.8 1.9 add_convert_fusion
  124.7 2.0 add_convert_fusion.2
  126.7 1.5 collective-permute-start.4
  128.2 1.5 collective-permute-start.5
  130.0 21.5 %attention_rear.1 = (bf16[2048,512]{1,0:T(8,128)(2,1)}, bf16[2048,512]{1,0:T(8,128)(2,1)}, f32[4,512]{1,0:T(4,128)}, f32[1,1024]{1,0:T(1,128)}) custom-call(s32[3]{0:T(128)} %pad_add_fusion.1.info, bf16[2048,512]{1,0:T(8,128)(2,1)} %get-tuple-element.115.fq_s, bf16[2048,512]{1,0:T(8,128)(2,1)} %get-tuple-element.116.fk_s, ...), custom_call_target="tpu_custom_call" | custom-call | flops 5153960960 | bytes 6710886 | tf_op jit(solution)/shard_map/attention_rear/pallas_call | solution.py:704
  151.5 0.8 collective-permute-done.5
  152.3 1.6 add_convert_fusion.11
  153.9 0.4 add_convert_fusion.10
  154.4 0.5 collective-permute-start.6
  155.3 0.1 concatenate.30
  155.4 0.7 copy.55
  156.1 16.8 %attn_weight_grads.1 = (bf16[8,128,512]{2,1,0:T(8,128)(2,1)}, bf16[8,128,512]{2,1,0:T(8,128)(2,1)}, bf16[8,136,512]{2,1,0:T(8,128)(2,1)}, bf16[8,136,512]{2,1,0:T(8,128)(2,1)}) custom-call(s32[2,16]{1,0:T(2,128)} %pad_add_fusion.table, bf16[2048,1024]{1,0:T(8,128)(2,1)} %get-tuple-element.102.normed, bf16[2048,512]{1,0:T(8,128)(2,1)} %get-tuple-element.134.attended, ...), custom_call_target="tpu_custom_call" | custom-call | flops 3435973888 | bytes 8388608 | tf_op jit(solution)/shard_map/attn_weight_grads/pallas_call | solution.py:359
  173.0 0.7 collective-permute-start.8
  173.7 1.4 collective-permute-start.7
  175.0 2.5 collective-permute-done.6
  177.5 0.4 add_convert_fusion.8
  177.9 2.6 collective-permute-start.9
  180.5 15.0 %back_rows.2 = bf16[1024,1024]{1,0:T(8,128)(2,1)} custom-call(s32[3]{0:T(128)} %pad_add_fusion.1.info, bf16[2048,512]{1,0:T(8,128)(2,1)} %get-tuple-element.135.dq, bf16[2048,512]{1,0:T(8,128)(2,1)} %get-tuple-element.136.dk, bf16[2048,512]{1,0:T(8,128)(2,1)} %get-tuple-element.137.dv, bf16[2048,2048]{1,0:T(8,128)(2,1)} %get-tuple-element.103.up_grad, ...), custom_call_target="tpu_custom_call" | custom-call | flops 3006477056 | bytes 8388608 | tf_op jit(solution)/shard_map/back_rows/pallas_call | solution.py:845
  195.5 1.0 collective-permute-done.7
  196.5 1.1 collective-permute-done.8
  197.7 0.3 add_convert_fusion.4
  198.0 0.3 add_convert_fusion.6
  198.3 1.4 collective-permute-start.11
  199.7 0.5 collective-permute-start.10
  200.3 11.8 %out_rows.2 = bf16[1024,1024]{1,0:T(8,128)(2,1)} custom-call(s32[3]{0:T(128)} %pad_add_fusion.1.info, bf16[2048,2048]{1,0:T(8,128)(2,1)} %get-tuple-element.100.act, bf16[2048,512]{1,0:T(8,128)(2,1)} %get-tuple-element.134.attended, bf16[1024,1024]{1,0:T(8,128)(2,1)} %w_proj.5, bf16[4096,1024]{1,0:T(8,128)(2,1)} %w_down.7), custom_call_target="tpu_custom_call" | custom-call | flops 2147483648 | bytes 5033164 | tf_op jit(solution)/shard_map/out_rows/pallas_call | solution.py:765
  212.1 0.2 add_bitcast_fusion
  212.3 1.5 collective-permute-done.10
  213.8 0.1 add_convert_fusion.18
  213.9 0.1 add_convert_fusion.14
  214.2 1.4 collective-permute-start.13
  215.5 17.4 %back_rows.3 = f32[1024,1024]{1,0:T(8,128)} custom-call(s32[3]{0:T(128)} %pad_add_fusion.1.info, bf16[2048,512]{1,0:T(8,128)(2,1)} %get-tuple-element.135.dq, bf16[2048,512]{1,0:T(8,128)(2,1)} %get-tuple-element.136.dk, bf16[2048,512]{1,0:T(8,128)(2,1)} %get-tuple-element.137.dv, bf16[2048,2048]{1,0:T(8,128)(2,1)} %get-tuple-element.103.up_grad, ...), custom_call_target="tpu_custom_call" | custom-call | flops 3006477056 | bytes 8388608 | tf_op jit(solution)/shard_map/back_rows/pallas_call | solution.py:845
  233.0 0.9 fusion.21
  233.9 0.3 collective-permute-start.17
  234.2 0.1 add_convert_fusion.16
  234.3 2.6 collective-permute-start.15
  237.0 0.2 copy.48
  237.2 0.2 reshape.96
  237.4 0.2 copy.49
  237.6 0.2 reshape.97
  237.9 0.4 copy.50
  238.3 0.4 reshape.98
  238.8 12.7 %out_rows.3 = bf16[1024,1024]{1,0:T(8,128)(2,1)} custom-call(s32[3]{0:T(128)} %pad_add_fusion.1.info, bf16[2048,2048]{1,0:T(8,128)(2,1)} %get-tuple-element.100.act, bf16[2048,512]{1,0:T(8,128)(2,1)} %get-tuple-element.134.attended, bf16[1024,1024]{1,0:T(8,128)(2,1)} %w_proj.5, bf16[4096,1024]{1,0:T(8,128)(2,1)} %w_down.7, bf16[1024,1024]{1,0:T(8,128)(2,1)} %rest_0_.3, ...), custom_call_target="tpu_custom_call" | custom-call | flops 2147483648 | bytes 5033164 | tf_op jit(solution)/shard_map/out_rows/pallas_call | solution.py:765
  251.8 3.1 %collective-permute-start.18 = (f32[32,1024]{1,0:T(8,128)S(1)}, f32[32,1024]{1,0:T(8,128)S(1)}, u32[]{:S(2)}, u32[]{:S(2)}) collective-permute-start(f32[32,1024]{1,0:T(8,128)S(1)} %pad_maximum_fusion.6), channel_id=1, source_target_pairs={{0,0},{1,16},{2,1},{3,17},{4,2},{5,18},{6,3},{7,19},{8,4},{9,20},{... | collective-permute-start | bytes 393224 | tf_op jit(solution)/shard_map/ppermute | solution.py:1061
  254.9 1.1 multiply_reduce_fusion
  256.0 6.3 %collective-permute-done.18 = f32[32,1024]{1,0:T(8,128)S(1)} collective-permute-done((f32[32,1024]{1,0:T(8,128)S(1)}, f32[32,1024]{1,0:T(8,128)S(1)}, u32[]{:S(2)}, u32[]{:S(2)}) %collective-permute-start.18) | collective-permute-done | bytes 131104 | tf_op jit(solution)/shard_map/ppermute | solution.py:1061
  262.5 0.5 fusion.17
  263.2 1.2 multiply_reduce_fusion.1
  264.6 0.5 fusion.15
  265.1 0.5 fusion.18
  265.6 1.3 convert_divide_fusion
  266.9 0.5 copy.70
  267.4 0.7 copy.71
  (83 shorter events, 1.7 us)
Async XLA Ops:
  0.6 26.1 %collective-permute-start = (bf16[1024,1024]{1,0:T(8,128)(2,1)}, bf16[1024,1024]{1,0:T(8,128)(2,1)}, u32[]{:S(2)}, u32[]{:S(2)}) collective-permute-start(bf16[1024,1024]{1,0:T(8,128)(2,1)} %rest_0_.3), channel_id=1, source_target_pairs={{0,1},{1,0},{2,3},{3,2},{4,5},{5,4},{6,7},{7,6},{8,9},{9,8},{10,11... | collective-permute-start | bytes 6291464 | tf_op jit(solution)/shard_map/ppermute | solution.py:955
  0.7 26.0 %collective-permute-start.1 = (bf16[1024,1024]{1,0:T(8,128)(2,1)}, bf16[1024,1024]{1,0:T(8,128)(2,1)}, u32[]{:S(2)}, u32[]{:S(2)}) collective-permute-start(bf16[1024,1024]{1,0:T(8,128)(2,1)} %cot.1), channel_id=1, source_target_pairs={{0,1},{1,0},{2,3},{3,2},{4,5},{5,4},{6,7},{7,6},{8,9},{9,8},{10,11... | collective-permute-start | bytes 6291464 | tf_op jit(solution)/shard_map/ppermute | solution.py:955
  74.7 47.9 %collective-permute-start.2 = (bf16[8,128,1024]{2,1,0:T(8,128)(2,1)}, bf16[8,128,1024]{2,1,0:T(8,128)(2,1)S(1)}, u32[]{:S(2)}, u32[]{:S(2)}) collective-permute-start(bf16[8,128,1024]{2,1,0:T(8,128)(2,1)} %get-tuple-element.108), channel_id=1, source_target_pairs={{0,2},{2,0},{4,6},{6,4},{8,10},{10,8},{12,14},{14,12},{16,18},{18,... | collective-permute-start | bytes 6291464 | tf_op jit(solution)/shard_map/ppermute | solution.py:889
  75.3 47.5 %collective-permute-start.3 = (bf16[8,128,1024]{2,1,0:T(8,128)(2,1)}, bf16[8,128,1024]{2,1,0:T(8,128)(2,1)S(1)}, u32[]{:S(2)}, u32[]{:S(2)}) collective-permute-start(bf16[8,128,1024]{2,1,0:T(8,128)(2,1)} %get-tuple-element.109), channel_id=1, source_target_pairs={{0,4},{2,6},{4,0},{6,2},{8,12},{10,14},{12,8},{14,10},{16,20},{18,... | collective-permute-start | bytes 6291464 | tf_op jit(solution)/shard_map/ppermute | solution.py:889
  76.8 46.0 %copy-start.1 = (bf16[8,128,1024]{2,1,0:T(8,128)(2,1)S(1)}, bf16[8,128,1024]{2,1,0:T(8,128)(2,1)}, u32[]{:S(2)}) copy-start(bf16[8,128,1024]{2,1,0:T(8,128)(2,1)} %get-tuple-element.111) | copy-start | bytes 6291460
  122.8 1.9 copy-start
  124.7 5.0 %copy-start.8 = (f32[1,1024]{1,0:T(1,128)S(1)}, f32[1,1024]{1,0:T(1,128)}, u32[]{:S(2)}) copy-start(f32[1,1024]{1,0:T(1,128)} %get-tuple-element.140) | copy-start | bytes 12292
  124.7 5.2 %copy-start.6 = (f32[1,2048]{1,0:T(1,128)S(1)}, f32[1,2048]{1,0:T(1,128)}, u32[]{:S(2)}) copy-start(f32[1,2048]{1,0:T(1,128)} %get-tuple-element.141) | copy-start | bytes 24580
  126.7 24.8 %collective-permute-start.4 = (bf16[4,128,1024]{2,1,0:T(8,128)(2,1)}, bf16[4,128,1024]{2,1,0:T(8,128)(2,1)}, u32[]{:S(2)}, u32[]{:S(2)}) collective-permute-start(bf16[4,128,1024]{2,1,0:T(8,128)(2,1)} %get-tuple-element.125), channel_id=1, source_target_pairs={{0,4},{2,6},{4,0},{6,2},{8,12},{10,14},{12,8},{14,10},{16,20},{18,... | collective-permute-start | bytes 3145736 | tf_op jit(solution)/shard_map/ppermute | solution.py:889
  128.2 24.0 %collective-permute-start.5 = (bf16[4,128,1024]{2,1,0:T(8,128)(2,1)}, bf16[4,128,1024]{2,1,0:T(8,128)(2,1)S(1)}, u32[]{:S(2)}, u32[]{:S(2)}) collective-permute-start(bf16[4,128,1024]{2,1,0:T(8,128)(2,1)} %get-tuple-element.126), channel_id=1, source_target_pairs={{0,2},{2,0},{4,6},{6,4},{8,10},{10,8},{12,14},{14,12},{16,18},{18,... | collective-permute-start | bytes 3145736 | tf_op jit(solution)/shard_map/ppermute | solution.py:889
  154.3 0.7 copy-start.7
  154.3 1.0 copy-start.9
  154.4 23.1 %collective-permute-start.6 = (bf16[2,256,1024]{2,1,0:T(8,128)(2,1)S(1)}, bf16[2,256,1024]{2,1,0:T(8,128)(2,1)S(1)}, u32[]{:S(2)}, u32[]{:S(2)}) collective-permute-start(bf16[2,256,1024]{2,1,0:T(8,128)(2,1)S(1)} %pad_maximum_fusion), channel_id=1, source_target_pairs={{0,8},{2,10},{4,12},{6,14},{8,0},{10,2},{12,4},{14,6},{16,24},{18,... | collective-permute-start | bytes 3145736 | tf_op jit(solution)/shard_map/ppermute | solution.py:889
  173.0 24.7 %collective-permute-start.8 = (bf16[8,136,512]{2,1,0:T(8,128)(2,1)}, bf16[8,136,512]{2,1,0:T(8,128)(2,1)S(1)}, u32[]{:S(2)}, u32[]{:S(2)}) collective-permute-start(bf16[8,136,512]{2,1,0:T(8,128)(2,1)} %get-tuple-element.144), channel_id=1, source_target_pairs={{0,4},{2,6},{4,0},{6,2},{8,12},{10,14},{12,8},{14,10},{16,20},{18,... | collective-permute-start | bytes 3342344 | tf_op jit(solution)/shard_map/ppermute | solution.py:889
  173.7 22.9 %collective-permute-start.7 = (bf16[8,128,512]{2,1,0:T(8,128)(2,1)}, bf16[8,128,512]{2,1,0:T(8,128)(2,1)S(1)}, u32[]{:S(2)}, u32[]{:S(2)}) collective-permute-start(bf16[8,128,512]{2,1,0:T(8,128)(2,1)} %get-tuple-element.143), channel_id=1, source_target_pairs={{0,2},{2,0},{4,6},{6,4},{8,10},{10,8},{12,14},{14,12},{16,18},{18,... | collective-permute-start | bytes 3145736 | tf_op jit(solution)/shard_map/ppermute | solution.py:889
  177.9 19.8 %copy-start.3 = (bf16[8,136,512]{2,1,0:T(8,128)(2,1)S(1)}, bf16[8,136,512]{2,1,0:T(8,128)(2,1)}, u32[]{:S(2)}) copy-start(bf16[8,136,512]{2,1,0:T(8,128)(2,1)} %get-tuple-element.146) | copy-start | bytes 3342340
  177.9 34.2 %collective-permute-start.9 = (bf16[1,256,1024]{2,1,0:T(8,128)(2,1)S(1)}, bf16[1,256,1024]{2,1,0:T(8,128)(2,1)S(1)}, u32[]{:S(2)}, u32[]{:S(2)}) collective-permute-start(bf16[1,256,1024]{2,1,0:T(8,128)(2,1)S(1)} %get-tuple-element.150), channel_id=1, source_target_pairs={{0,16},{2,18},{4,20},{6,22},{8,24},{10,26},{12,28},{14,30},{16,0},... | collective-permute-start | bytes 1572872 | tf_op jit(solution)/shard_map/ppermute | solution.py:889
  195.5 2.5 copy-start.4
  197.7 17.9 %collective-permute-start.12 = (bf16[1024,1024]{1,0:T(8,128)(2,1)}, bf16[1024,1024]{1,0:T(8,128)(2,1)}, u32[]{:S(2)}, u32[]{:S(2)}) collective-permute-start(bf16[1024,1024]{1,0:T(8,128)(2,1)} %back_rows.2), channel_id=1, source_target_pairs={{0,1},{1,0},{2,3},{3,2},{4,5},{5,4},{6,7},{7,6},{8,9},{9,8},{10,11... | collective-permute-start | bytes 6291464 | tf_op jit(solution)/shard_map/ppermute | solution.py:955
  198.3 15.5 %collective-permute-start.11 = (bf16[4,136,512]{2,1,0:T(8,128)(2,1)S(1)}, bf16[4,136,512]{2,1,0:T(8,128)(2,1)S(1)}, u32[]{:S(2)}, u32[]{:S(2)}) collective-permute-start(bf16[4,136,512]{2,1,0:T(8,128)(2,1)S(1)} %get-tuple-element.156), channel_id=1, source_target_pairs={{0,2},{2,0},{4,6},{6,4},{8,10},{10,8},{12,14},{14,12},{16,18},{18,... | collective-permute-start | bytes 1671176 | tf_op jit(solution)/shard_map/ppermute | solution.py:889
  199.7 14.1 %collective-permute-start.10 = (bf16[4,128,512]{2,1,0:T(8,128)(2,1)S(1)}, bf16[4,128,512]{2,1,0:T(8,128)(2,1)S(1)}, u32[]{:S(2)}, u32[]{:S(2)}) collective-permute-start(bf16[4,128,512]{2,1,0:T(8,128)(2,1)S(1)} %get-tuple-element.155), channel_id=1, source_target_pairs={{0,4},{2,6},{4,0},{6,2},{8,12},{10,14},{12,8},{14,10},{16,20},{18,... | collective-permute-start | bytes 1572872 | tf_op jit(solution)/shard_map/ppermute | solution.py:889
  213.8 25.0 %collective-permute-start.14 = (bf16[1024,1024]{1,0:T(8,128)(2,1)}, bf16[1024,1024]{1,0:T(8,128)(2,1)}, u32[]{:S(2)}, u32[]{:S(2)}) collective-permute-start(bf16[1024,1024]{1,0:T(8,128)(2,1)} %out_rows.2), channel_id=1, source_target_pairs={{0,1},{1,0},{2,3},{3,2},{4,5},{5,4},{6,7},{7,6},{8,9},{9,8},{10,11... | collective-permute-start | bytes 6291464 | tf_op jit(solution)/shard_map/ppermute | solution.py:955
  214.2 18.8 %collective-permute-start.13 = (bf16[2,264,512]{2,1,0:T(8,128)(2,1)S(1)}, bf16[2,264,512]{2,1,0:T(8,128)(2,1)S(1)}, u32[]{:S(2)}, u32[]{:S(2)}) collective-permute-start(bf16[2,264,512]{2,1,0:T(8,128)(2,1)S(1)} %pad_maximum_fusion.2), channel_id=1, source_target_pairs={{0,8},{2,10},{4,12},{6,14},{8,0},{10,2},{12,4},{14,6},{16,24},{18,... | collective-permute-start | bytes 1622024 | tf_op jit(solution)/shard_map/ppermute | solution.py:889
  233.9 3.0 %collective-permute-start.17 = (f32[2,32,1024]{2,1,0:T(8,128)S(1)}, f32[2,32,1024]{2,1,0:T(8,128)S(1)}, u32[]{:S(2)}, u32[]{:S(2)}) collective-permute-start(f32[2,32,1024]{2,1,0:T(8,128)S(1)} %dynamic-slice_bitcast_fusion), channel_id=1, source_target_pairs={{0,1},{1,0},{2,3},{3,2},{4,5},{5,4},{6,7},{7,6},{8,9},{9,8},{10,11... | collective-permute-start | bytes 786440 | tf_op jit(solution)/shard_map/ppermute | solution.py:955
  234.3 17.1 %collective-permute-start.15 = (bf16[1,264,512]{2,1,0:T(8,128)(2,1)S(1)}, bf16[1,264,512]{2,1,0:T(8,128)(2,1)S(1)}, u32[]{:S(2)}, u32[]{:S(2)}) collective-permute-start(bf16[1,264,512]{2,1,0:T(8,128)(2,1)S(1)} %get-tuple-element.167), channel_id=1, source_target_pairs={{0,16},{2,18},{4,20},{6,22},{8,24},{10,26},{12,28},{14,30},{16,0},... | collective-permute-start | bytes 811016 | tf_op jit(solution)/shard_map/ppermute | solution.py:889
  238.7 16.2 %copy-start.2 = (f32[32,4096]{1,0:T(8,128)}, f32[32,4096]{1,0:T(8,128)S(1)}, u32[]{:S(2)}) copy-start(f32[32,4096]{1,0:T(8,128)S(1)} %reshape.98) | copy-start | bytes 1572868
  251.7 10.7 %collective-permute-start.16 = (f32[104,512]{1,0:T(8,128)S(1)}, f32[104,512]{1,0:T(8,128)S(1)}, u32[]{:S(2)}, u32[]{:S(2)}) collective-permute-start(f32[104,512]{1,0:T(8,128)S(1)} %pad_maximum_fusion.5), channel_id=1, source_target_pairs={{0,1},{1,0},{2,3},{3,2},{4,5},{5,4},{6,7},{7,6},{8,9},{9,8},{10,11... | collective-permute-start | bytes 638984 | tf_op jit(solution)/shard_map/ppermute | solution.py:955
  251.8 10.6 %collective-permute-start.18 = (f32[32,1024]{1,0:T(8,128)S(1)}, f32[32,1024]{1,0:T(8,128)S(1)}, u32[]{:S(2)}, u32[]{:S(2)}) collective-permute-start(f32[32,1024]{1,0:T(8,128)S(1)} %pad_maximum_fusion.6), channel_id=1, source_target_pairs={{0,0},{1,16},{2,1},{3,17},{4,2},{5,18},{6,3},{7,19},{8,4},{9,20},{... | collective-permute-start | bytes 393224 | tf_op jit(solution)/shard_map/ppermute | solution.py:1061
  262.5 5.6 %copy-start.10 = (f32[32]{0:T(128)}, f32[32]{0:T(128)S(1)}, u32[]{:S(2)}) copy-start(f32[32]{0:T(128)S(1)} %fusion.16) | copy-start | bytes 388
  263.2 4.9 %copy-start.5 = (f32[32,3072]{1,0:T(8,128)}, f32[32,3072]{1,0:T(8,128)S(1)}, u32[]{:S(2)}) copy-start(f32[32,3072]{1,0:T(8,128)S(1)} %fusion.2) | copy-start | bytes 1179652

commit v2 on v1

--- a/solution.py
+++ b/solution.py
@@ -110,6 +110,7 @@
             sums[...] = jnp.zeros_like(sums)
         else:
             upb[...] = rest[4][...]
+            sums[...] = jnp.zeros_like(sums)
 
     rows = res.shape[0]
     xhat, _ = norm_stats(res[...].astype(F32))
@@ -155,17 +156,6 @@
         grad = (back * (phi + up * bell)).astype(BF)
         up_grad[:, cols] = grad
         upb[:, cols] += mm(ones, grad)[0:1]
-
-    if half == 1:
-
-        @pl.when(step == tiles - 1)
-        def _():
-            sums[...] = jnp.zeros_like(sums)
-
-            @pl.loop(0, upb.shape[1] // (2 * GROUP))
-            def _(j):
-                cols = pl.ds(pl.multiple_of(j * 2 * GROUP, GROUP), 2 * GROUP)
-                sums[...] += exact_row(upb[:, cols], up_buf[:, cols])
 
 
 def mlp_rows(half, info, res, cot, vectors, w_up, w_down, earlier=()):
@@ -433,10 +423,11 @@
 
 
 def attn_front_kernel(
-    info, normed, target, w_q, w_k, w_v, b_q, b_k, b_v, w_proj, scale, mix_high, mix_low, base, inner,
-    attended, dq, fq_s, fk_s, v_s, tk_s, gn_s, gx_s, bias_q, scale_grad, state, total,
+    info, normed, target, w_q, w_k, w_v, b_q, b_k, b_v, w_proj, scale, mix_high, mix_low, base, inner, upb, w_up,
+    attended, dq, fq_s, fk_s, v_s, tk_s, gn_s, gx_s, bias_q, scale_grad, shift, state, total, up_buf, sems,
 ):
     step = pl.program_id(0)
+    strips = up_buf.shape[1] // LANES
     groups = w_q.shape[1] // GROUP
     span = TILE // CHUNK
     stack_mask, block_mask = patterns()
@@ -452,8 +443,12 @@
 
     @pl.when(step == 0)
     def _():
-        for item in (state, total, bias_q, scale_grad):
+        for item in (state, total, bias_q, scale_grad, shift):
             item[...] = jnp.zeros_like(item)
+
+        @pl.loop(0, strips)
+        def _(j):
+            strip_copy(info[0], w_up, up_buf, sems, 0, j).start()
 
     x = normed[...]
     cosine, low, high = tables(base, inner, step)
@@ -522,6 +517,17 @@
 
     interleave([feature(g, which) for g in range(groups) for which in range(2)], 0)
     interleave([unit(g, c) for c in range(span) for g in range(groups)], 0)
+
+    @pl.when(step == pl.num_programs(0) - 1)
+    def _():
+        @pl.loop(0, strips)
+        def _(j):
+            strip_copy(info[0], w_up, up_buf, sems, 0, j).wait()
+
+        @pl.loop(0, upb.shape[1] // GROUP)
+        def _(j):
+            cols = pl.ds(pl.multiple_of(j * GROUP, GROUP), GROUP)
+            shift[...] += exact_row(upb[:, cols], up_buf[:, cols])
 
 
 def attn_rear_kernel(
@@ -653,8 +659,9 @@
     return ((tile // own) ^ info[0]) * own + tile % own
 
 
-def attention_front(info, normed, target, w_qkv, w_proj, vectors, mix, turns):
+def attention_front(info, normed, target, w_qkv, w_proj, vectors, mix, turns, upb, w_up):
     total, dim = normed.shape
+    ff = upb.shape[1]
     half = dim // 2
     tiles = total // TILE
     front = lambda i, info: (stored(i, info, tiles // 2), 0)
@@ -666,6 +673,7 @@
         out_shape=(
             *(jax.ShapeDtypeStruct((total, half), BF) for _ in range(8)),
             *(jax.ShapeDtypeStruct((1, half), F32) for _ in range(2)),
+            jax.ShapeDtypeStruct((1, dim), F32),
         ),
         grid_spec=pltpu.PrefetchScalarGridSpec(
             num_scalar_prefetch=1,
@@ -682,16 +690,23 @@
                 pl.BlockSpec((half, dim), lambda i, info: (info[0], 0), pipeline_mode=pl.Buffered(1)),
                 vector_spec(half, 2 * dim, 0),
             ]
-            + [whole(item.shape) for item in (*mix, *turns)],
+            + [whole(item.shape) for item in (*mix, *turns, upb)]
+            + [anywhere()],
             out_specs=[pl.BlockSpec((TILE, half), front)] * 2
             + [pl.BlockSpec((TILE, half), plain)] * 6
-            + [whole((1, half))] * 2,
-            scratch_shapes=[pltpu.VMEM((groups, GROUP, GROUP), F32), pltpu.VMEM((groups, 1, GROUP), F32)],
+            + [whole((1, half))] * 2
+            + [whole((1, dim))],
+            scratch_shapes=[
+                pltpu.VMEM((groups, GROUP, GROUP), F32),
+                pltpu.VMEM((groups, 1, GROUP), F32),
+                pltpu.VMEM((dim, ff), BF),
+                pltpu.SemaphoreType.DMA((1, ff // LANES)),
+            ],
         ),
         compiler_params=params(),
         cost_estimate=cost(8 * total * dim * half + 64 * total * half * GROUP, 12 * total * dim, 2 * total * half),
         name="attention_front",
-    )(info, normed, target, w_qkv, w_qkv, w_qkv, vectors, vectors, vectors, w_proj, vectors, *mix, *turns)
+    )(info, normed, target, w_qkv, w_qkv, w_qkv, vectors, vectors, vectors, w_proj, vectors, *mix, *turns, upb, w_up)
 
 
 def attention_rear(info, saved, bias_q, scale_sum, w_qkv, vectors, shift, mix, turns):
@@ -971,7 +986,7 @@
     other_res = swap(residual)
     other_cot = swap(cotangent)
     *mine, target_sum = mlp_rows(0, info, residual, cotangent, vectors, w_up, w_down)
-    normed, target, act, up_grad, upb, shift = mlp_rows(
+    normed, target, act, up_grad, upb, _ = mlp_rows(
         1, info, other_res, other_cot, vectors, w_up, w_down, mine
     )
 
@@ -979,8 +994,8 @@
     parts = mlp_weight_grads(ndp, table, act, target, normed, up_grad)
     mlp_sums = Reduction(parts[:2], parts[2:], ndp)
 
-    attended, dq, *saved, bias_q, scale_sum = attention_front(
-        info, normed, target, w_qkv, w_proj, vectors, mix, turns
+    attended, dq, *saved, bias_q, scale_sum, shift = attention_front(
+        info, normed, target, w_qkv, w_proj, vectors, mix, turns, upb, w_up
     )
     attended = mlp_sums.land(attended)
     info = mlp_sums.after(info)

time: 269 us -> 267 us (level)
  waiting for transfers between devices: 16.7 us -> 12.5 us
    ppermute x12, waiting for transfers between devices: 10.3 us -> 6.84 us  [cross(): return lax.ppermute(value, 'dp', [(i, i ^ bit) for i in range(ndp)])]
    pallas_call x1, Pallas kernels: 42.6 us -> 45.6 us  [attention_front(): pl.pallas_call(attn_front_kernel, out_shape=(*(jax.ShapeDtypeStruct((tota...]
  transfers between devices with their start and end apart: 19 -> 19, of which waited for: 8 -> 8; matrix products, arithmetic and copies ran while one was open for 3% -> 3% of each run, Pallas kernels for 60% -> 62%
where the time goes in v2:
time: 267 us; the launch traced here: 266 us
  Pallas kernels  211 us (79%)
  starting transfers between devices  21 us (8%)
  other arithmetic  12.9 us (5%)
  waiting for transfers between devices  12.5 us (5%)
  local copies, waits for them, and re-layouts  6.97 us (3%)
    pallas_call x1, Pallas kernels, attention_front(): pl.pallas_call(attn_front_kernel, out_shape=(*(jax.ShapeDtypeStruct((tota...  45.6 us
    pallas_call x2, Pallas kernels, mlp_rows(): pl.pallas_call(partial(mlp_kernel, half, tiles), out_shape=outs, grid_spe...  43.6 us
    pallas_call x2, Pallas kernels, back_rows(): pl.pallas_call(partial(back_kernel, own), out_shape=jax.ShapeDtypeStruct(...  32.5 us
    pallas_call x1, Pallas kernels, mlp_weight_grads(): pl.pallas_call(partial(mlp_grad_kernel, tiles), out_shape=(shape,) * 4, g...  24.6 us
    pallas_call x2, Pallas kernels, out_rows(): pl.pallas_call(partial(out_kernel, own), out_shape=jax.ShapeDtypeStruct((...  24.5 us
    pallas_call x1, Pallas kernels, attention_rear(): pl.pallas_call(partial(attn_rear_kernel, tiles), out_shape=(*(jax.ShapeDt...  21.5 us
    pallas_call x1, Pallas kernels, attn_weight_grads(): pl.pallas_call(attn_grad_kernel, out_shape=(shapes[0], shapes[0], shapes[...  16.8 us
    ppermute x12, starting transfers between devices, cross(): return lax.ppermute(value, 'dp', [(i, i ^ bit) for i in range(ndp)])  16.6 us
  transfers between devices with their start and end apart: 19, of which 8 were waited for; matrix products, arithmetic and copies ran while one was open for 3% of the time, Pallas kernels for 62%

profile of v2, /device:TPU:10, one launch (start us, length us, event | category | flops | bytes accessed | tf_op | source)
XLA Modules:
  0.0 266.2 jit_solution(7294866852849871199)
XLA Ops:
  0.7 0.5 collective-permute-start.1
  1.9 1.9 prepare.1
  3.7 0.6 pad_add_fusion.1.info
  4.3 0.6 pad_add_fusion.table
  4.9 21.8 %mlp_rows.2 = (bf16[2048,1024]{1,0:T(8,128)(2,1)}, bf16[2048,1024]{1,0:T(8,128)(2,1)}, bf16[2048,2048]{1,0:T(8,128)(2,1)}, bf16[2048,2048]{1,0:T(8,128)(2,1)}, f32[1,2048]{1,0:T(1,128)}, /*index=5*/f32[1,1024]{1,0:T(1,128)}) custom-call(s32[3]{0:T(128)} %pad_add_fusion.1.info, bf16[1024,1024]{1,0:T(8,128)(2,1)} %rest_0_.3, bf16[1024,1024]{1,0:T(8,128)(2,1)} %cot.1, ...), custom_call_target="tpu_custom_call" | custom-call | flops 3435973888 | bytes 18454936 | tf_op jit(solution)/shard_map/mlp_rows/pallas_call | solution.py:177
  26.7 21.8 %mlp_rows.3 = (bf16[2048,1024]{1,0:T(8,128)(2,1)}, bf16[2048,1024]{1,0:T(8,128)(2,1)}, bf16[2048,2048]{1,0:T(8,128)(2,1)}, bf16[2048,2048]{1,0:T(8,128)(2,1)}, f32[1,2048]{1,0:T(1,128)}, /*index=5*/f32[1,1024]{1,0:T(1,128)}) custom-call(s32[3]{0:T(128)} %pad_add_fusion.1.info, ...), custom_call_target="tpu_custom_call", output_to_operand_aliasing={{0}: (8, {}), {1}: (9, {}), {2}: (10, {}), {3}: (11, {})} | custom-call | flops 3435973888 | bytes 18454936 | tf_op jit(solution)/shard_map/mlp_rows/pallas_call | solution.py:177
  48.6 24.6 %mlp_weight_grads.1 = (bf16[8,128,1024]{2,1,0:T(8,128)(2,1)}, bf16[8,128,1024]{2,1,0:T(8,128)(2,1)}, bf16[8,128,1024]{2,1,0:T(8,128)(2,1)}, bf16[8,128,1024]{2,1,0:T(8,128)(2,1)}) custom-call(s32[2,16]{1,0:T(2,128)} %pad_add_fusion.table, bf16[2048,2048]{1,0:T(8,128)(2,1)} %get-tuple-element.100.act, bf16[2048,1024]{1,0:T(8,128)(2,1)} %get-tuple-element.101.target.rest_2_, ...), custom_call_target="tpu_custom_call" | custom-call | flops 6871947776 | bytes 13421772 | tf_op jit(solution)/shard_map/mlp_weight_grads/pallas_call | solution.py:285
  73.2 0.6 collective-permute-start.2
  73.8 1.5 collective-permute-start.3
  75.3 45.6 %attention_front.1 = (bf16[2048,512]{1,0:T(8,128)(2,1)}, bf16[2048,512]{1,0:T(8,128)(2,1)}, bf16[2048,512]{1,0:T(8,128)(2,1)}, bf16[2048,512]{1,0:T(8,128)(2,1)}...) custom-call(s32[3]{0:T(128)} %pad_add_fusion.1.info, ...), custom_call_target="tpu_custom_call" | custom-call | flops 10307921920 | bytes 10066329 | tf_op jit(solution)/shard_map/attention_front/pallas_call | solution.py:671
  120.9 0.2 collective-permute-done.2
  121.1 0.2 collective-permute-done.3
  121.3 1.9 add_convert_fusion
  123.2 2.0 add_convert_fusion.2
  125.2 1.5 collective-permute-start.4
  126.7 1.5 collective-permute-start.5
  128.5 21.5 %attention_rear.1 = (bf16[2048,512]{1,0:T(8,128)(2,1)}, bf16[2048,512]{1,0:T(8,128)(2,1)}, f32[4,512]{1,0:T(4,128)}, f32[1,1024]{1,0:T(1,128)}) custom-call(s32[3]{0:T(128)} %pad_add_fusion.1.info, bf16[2048,512]{1,0:T(8,128)(2,1)} %get-tuple-element.116.fq_s, bf16[2048,512]{1,0:T(8,128)(2,1)} %get-tuple-element.117.fk_s, ...), custom_call_target="tpu_custom_call" | custom-call | flops 5153960960 | bytes 6710886 | tf_op jit(solution)/shard_map/attention_rear/pallas_call | solution.py:719
  150.0 0.8 collective-permute-done.5
  150.8 1.6 add_convert_fusion.11
  152.4 0.4 add_convert_fusion.10
  152.9 0.5 collective-permute-start.6
  153.8 0.1 concatenate.30
  153.9 0.7 copy.55
  154.6 16.8 %attn_weight_grads.1 = (bf16[8,128,512]{2,1,0:T(8,128)(2,1)}, bf16[8,128,512]{2,1,0:T(8,128)(2,1)}, bf16[8,136,512]{2,1,0:T(8,128)(2,1)}, bf16[8,136,512]{2,1,0:T(8,128)(2,1)}) custom-call(s32[2,16]{1,0:T(2,128)} %pad_add_fusion.table, bf16[2048,1024]{1,0:T(8,128)(2,1)} %get-tuple-element.102.normed, bf16[2048,512]{1,0:T(8,128)(2,1)} %get-tuple-element.135.attended, ...), custom_call_target="tpu_custom_call" | custom-call | flops 3435973888 | bytes 8388608 | tf_op jit(solution)/shard_map/attn_weight_grads/pallas_call | solution.py:349
  171.5 0.7 collective-permute-start.8
  172.2 1.5 collective-permute-start.7
  173.7 2.3 collective-permute-done.6
  176.0 0.4 add_convert_fusion.8
  176.4 2.6 collective-permute-start.9
  179.0 15.0 %back_rows.2 = bf16[1024,1024]{1,0:T(8,128)(2,1)} custom-call(s32[3]{0:T(128)} %pad_add_fusion.1.info, bf16[2048,512]{1,0:T(8,128)(2,1)} %get-tuple-element.136.dq, bf16[2048,512]{1,0:T(8,128)(2,1)} %get-tuple-element.137.dk, bf16[2048,512]{1,0:T(8,128)(2,1)} %get-tuple-element.138.dv, bf16[2048,2048]{1,0:T(8,128)(2,1)} %get-tuple-element.103.up_grad, ...), custom_call_target="tpu_custom_call" | custom-call | flops 3006477056 | bytes 8388608 | tf_op jit(solution)/shard_map/back_rows/pallas_call | solution.py:860
  194.0 1.2 collective-permute-done.7
  195.2 1.0 collective-permute-done.8
  196.2 0.3 add_convert_fusion.4
  196.5 0.3 add_convert_fusion.6
  196.8 1.4 collective-permute-start.11
  198.2 0.8 collective-permute-start.10
  199.1 11.8 %out_rows.2 = bf16[1024,1024]{1,0:T(8,128)(2,1)} custom-call(s32[3]{0:T(128)} %pad_add_fusion.1.info, bf16[2048,2048]{1,0:T(8,128)(2,1)} %get-tuple-element.100.act, bf16[2048,512]{1,0:T(8,128)(2,1)} %get-tuple-element.135.attended, bf16[1024,1024]{1,0:T(8,128)(2,1)} %w_proj.5, bf16[4096,1024]{1,0:T(8,128)(2,1)} %w_down.7), custom_call_target="tpu_custom_call" | custom-call | flops 2147483648 | bytes 5033164 | tf_op jit(solution)/shard_map/out_rows/pallas_call | solution.py:780
  210.9 0.2 add_bitcast_fusion
  211.1 1.2 collective-permute-done.10
  212.3 0.1 add_convert_fusion.18
  212.4 0.1 add_convert_fusion.14
  212.7 1.4 collective-permute-start.13
  214.0 17.4 %back_rows.3 = f32[1024,1024]{1,0:T(8,128)} custom-call(s32[3]{0:T(128)} %pad_add_fusion.1.info, bf16[2048,512]{1,0:T(8,128)(2,1)} %get-tuple-element.136.dq, bf16[2048,512]{1,0:T(8,128)(2,1)} %get-tuple-element.137.dk, bf16[2048,512]{1,0:T(8,128)(2,1)} %get-tuple-element.138.dv, bf16[2048,2048]{1,0:T(8,128)(2,1)} %get-tuple-element.103.up_grad, ...), custom_call_target="tpu_custom_call" | custom-call | flops 3006477056 | bytes 8388608 | tf_op jit(solution)/shard_map/back_rows/pallas_call | solution.py:860
  231.5 0.9 fusion.21
  232.4 0.3 collective-permute-start.17
  232.7 0.1 add_convert_fusion.16
  232.8 2.6 collective-permute-start.15
  235.5 0.2 copy.48
  235.7 0.2 reshape.96
  235.9 0.2 copy.49
  236.1 0.2 reshape.97
  236.4 0.4 copy.50
  236.8 0.4 reshape.98
  237.3 12.7 %out_rows.3 = bf16[1024,1024]{1,0:T(8,128)(2,1)} custom-call(s32[3]{0:T(128)} %pad_add_fusion.1.info, bf16[2048,2048]{1,0:T(8,128)(2,1)} %get-tuple-element.100.act, bf16[2048,512]{1,0:T(8,128)(2,1)} %get-tuple-element.135.attended, bf16[1024,1024]{1,0:T(8,128)(2,1)} %w_proj.5, bf16[4096,1024]{1,0:T(8,128)(2,1)} %w_down.7, bf16[1024,1024]{1,0:T(8,128)(2,1)} %rest_0_.3, ...), custom_call_target="tpu_custom_call" | custom-call | flops 2147483648 | bytes 5033164 | tf_op jit(solution)/shard_map/out_rows/pallas_call | solution.py:780
  250.3 3.5 %collective-permute-start.18 = (f32[32,1024]{1,0:T(8,128)S(1)}, f32[32,1024]{1,0:T(8,128)S(1)}, u32[]{:S(2)}, u32[]{:S(2)}) collective-permute-start(f32[32,1024]{1,0:T(8,128)S(1)} %pad_maximum_fusion.6), channel_id=1, source_target_pairs={{0,0},{1,16},{2,1},{3,17},{4,2},{5,18},{6,3},{7,19},{8,4},{9,20},{... | collective-permute-start | bytes 393224 | tf_op jit(solution)/shard_map/ppermute | solution.py:1076
  253.8 1.1 multiply_reduce_fusion
  254.9 5.6 %collective-permute-done.18 = f32[32,1024]{1,0:T(8,128)S(1)} collective-permute-done((f32[32,1024]{1,0:T(8,128)S(1)}, f32[32,1024]{1,0:T(8,128)S(1)}, u32[]{:S(2)}, u32[]{:S(2)}) %collective-permute-start.18) | collective-permute-done | bytes 131104 | tf_op jit(solution)/shard_map/ppermute | solution.py:1076
  260.6 0.5 fusion.17
  261.3 1.2 multiply_reduce_fusion.1
  262.7 0.5 fusion.15
  263.2 0.5 fusion.18
  263.7 1.3 convert_divide_fusion
  265.0 0.5 copy.70
  265.5 0.7 copy.71
  (83 shorter events, 1.7 us)
Async XLA Ops:
  0.6 26.1 %collective-permute-start = (bf16[1024,1024]{1,0:T(8,128)(2,1)}, bf16[1024,1024]{1,0:T(8,128)(2,1)}, u32[]{:S(2)}, u32[]{:S(2)}) collective-permute-start(bf16[1024,1024]{1,0:T(8,128)(2,1)} %rest_0_.3), channel_id=1, source_target_pairs={{0,1},{1,0},{2,3},{3,2},{4,5},{5,4},{6,7},{7,6},{8,9},{9,8},{10,11... | collective-permute-start | bytes 6291464 | tf_op jit(solution)/shard_map/ppermute | solution.py:970
  0.7 26.0 %collective-permute-start.1 = (bf16[1024,1024]{1,0:T(8,128)(2,1)}, bf16[1024,1024]{1,0:T(8,128)(2,1)}, u32[]{:S(2)}, u32[]{:S(2)}) collective-permute-start(bf16[1024,1024]{1,0:T(8,128)(2,1)} %cot.1), channel_id=1, source_target_pairs={{0,1},{1,0},{2,3},{3,2},{4,5},{5,4},{6,7},{7,6},{8,9},{9,8},{10,11... | collective-permute-start | bytes 6291464 | tf_op jit(solution)/shard_map/ppermute | solution.py:970
  73.2 47.9 %collective-permute-start.2 = (bf16[8,128,1024]{2,1,0:T(8,128)(2,1)}, bf16[8,128,1024]{2,1,0:T(8,128)(2,1)S(1)}, u32[]{:S(2)}, u32[]{:S(2)}) collective-permute-start(bf16[8,128,1024]{2,1,0:T(8,128)(2,1)} %get-tuple-element.109), channel_id=1, source_target_pairs={{0,2},{2,0},{4,6},{6,4},{8,10},{10,8},{12,14},{14,12},{16,18},{18,... | collective-permute-start | bytes 6291464 | tf_op jit(solution)/shard_map/ppermute | solution.py:904
  73.8 47.5 %collective-permute-start.3 = (bf16[8,128,1024]{2,1,0:T(8,128)(2,1)}, bf16[8,128,1024]{2,1,0:T(8,128)(2,1)S(1)}, u32[]{:S(2)}, u32[]{:S(2)}) collective-permute-start(bf16[8,128,1024]{2,1,0:T(8,128)(2,1)} %get-tuple-element.110), channel_id=1, source_target_pairs={{0,4},{2,6},{4,0},{6,2},{8,12},{10,14},{12,8},{14,10},{16,20},{18,... | collective-permute-start | bytes 6291464 | tf_op jit(solution)/shard_map/ppermute | solution.py:904
  75.3 46.0 %copy-start.1 = (bf16[8,128,1024]{2,1,0:T(8,128)(2,1)S(1)}, bf16[8,128,1024]{2,1,0:T(8,128)(2,1)}, u32[]{:S(2)}) copy-start(bf16[8,128,1024]{2,1,0:T(8,128)(2,1)} %get-tuple-element.112) | copy-start | bytes 6291460
  121.3 1.9 copy-start
  123.2 5.0 %copy-start.8 = (f32[1,1024]{1,0:T(1,128)S(1)}, f32[1,1024]{1,0:T(1,128)}, u32[]{:S(2)}) copy-start(f32[1,1024]{1,0:T(1,128)} %get-tuple-element.141) | copy-start | bytes 12292
  123.2 5.2 %copy-start.6 = (f32[1,2048]{1,0:T(1,128)S(1)}, f32[1,2048]{1,0:T(1,128)}, u32[]{:S(2)}) copy-start(f32[1,2048]{1,0:T(1,128)} %get-tuple-element.107.upb) | copy-start | bytes 24580
  125.2 24.8 %collective-permute-start.4 = (bf16[4,128,1024]{2,1,0:T(8,128)(2,1)}, bf16[4,128,1024]{2,1,0:T(8,128)(2,1)}, u32[]{:S(2)}, u32[]{:S(2)}) collective-permute-start(bf16[4,128,1024]{2,1,0:T(8,128)(2,1)} %get-tuple-element.126), channel_id=1, source_target_pairs={{0,4},{2,6},{4,0},{6,2},{8,12},{10,14},{12,8},{14,10},{16,20},{18,... | collective-permute-start | bytes 3145736 | tf_op jit(solution)/shard_map/ppermute | solution.py:904
  126.7 24.0 %collective-permute-start.5 = (bf16[4,128,1024]{2,1,0:T(8,128)(2,1)}, bf16[4,128,1024]{2,1,0:T(8,128)(2,1)S(1)}, u32[]{:S(2)}, u32[]{:S(2)}) collective-permute-start(bf16[4,128,1024]{2,1,0:T(8,128)(2,1)} %get-tuple-element.127), channel_id=1, source_target_pairs={{0,2},{2,0},{4,6},{6,4},{8,10},{10,8},{12,14},{14,12},{16,18},{18,... | collective-permute-start | bytes 3145736 | tf_op jit(solution)/shard_map/ppermute | solution.py:904
  152.8 0.7 copy-start.7
  152.8 1.0 copy-start.9
  152.9 23.1 %collective-permute-start.6 = (bf16[2,256,1024]{2,1,0:T(8,128)(2,1)S(1)}, bf16[2,256,1024]{2,1,0:T(8,128)(2,1)S(1)}, u32[]{:S(2)}, u32[]{:S(2)}) collective-permute-start(bf16[2,256,1024]{2,1,0:T(8,128)(2,1)S(1)} %pad_maximum_fusion), channel_id=1, source_target_pairs={{0,8},{2,10},{4,12},{6,14},{8,0},{10,2},{12,4},{14,6},{16,24},{18,... | collective-permute-start | bytes 3145736 | tf_op jit(solution)/shard_map/ppermute | solution.py:904
  171.5 24.7 %collective-permute-start.8 = (bf16[8,136,512]{2,1,0:T(8,128)(2,1)}, bf16[8,136,512]{2,1,0:T(8,128)(2,1)S(1)}, u32[]{:S(2)}, u32[]{:S(2)}) collective-permute-start(bf16[8,136,512]{2,1,0:T(8,128)(2,1)} %get-tuple-element.144), channel_id=1, source_target_pairs={{0,4},{2,6},{4,0},{6,2},{8,12},{10,14},{12,8},{14,10},{16,20},{18,... | collective-permute-start | bytes 3342344 | tf_op jit(solution)/shard_map/ppermute | solution.py:904
  172.2 23.0 %collective-permute-start.7 = (bf16[8,128,512]{2,1,0:T(8,128)(2,1)}, bf16[8,128,512]{2,1,0:T(8,128)(2,1)S(1)}, u32[]{:S(2)}, u32[]{:S(2)}) collective-permute-start(bf16[8,128,512]{2,1,0:T(8,128)(2,1)} %get-tuple-element.143), channel_id=1, source_target_pairs={{0,2},{2,0},{4,6},{6,4},{8,10},{10,8},{12,14},{14,12},{16,18},{18,... | collective-permute-start | bytes 3145736 | tf_op jit(solution)/shard_map/ppermute | solution.py:904
  176.4 19.8 %copy-start.3 = (bf16[8,136,512]{2,1,0:T(8,128)(2,1)S(1)}, bf16[8,136,512]{2,1,0:T(8,128)(2,1)}, u32[]{:S(2)}) copy-start(bf16[8,136,512]{2,1,0:T(8,128)(2,1)} %get-tuple-element.146) | copy-start | bytes 3342340
  176.4 34.5 %collective-permute-start.9 = (bf16[1,256,1024]{2,1,0:T(8,128)(2,1)S(1)}, bf16[1,256,1024]{2,1,0:T(8,128)(2,1)S(1)}, u32[]{:S(2)}, u32[]{:S(2)}) collective-permute-start(bf16[1,256,1024]{2,1,0:T(8,128)(2,1)S(1)} %get-tuple-element.150), channel_id=1, source_target_pairs={{0,16},{2,18},{4,20},{6,22},{8,24},{10,26},{12,28},{14,30},{16,0},... | collective-permute-start | bytes 1572872 | tf_op jit(solution)/shard_map/ppermute | solution.py:904
  194.0 2.5 copy-start.4
  196.2 17.9 %collective-permute-start.12 = (bf16[1024,1024]{1,0:T(8,128)(2,1)}, bf16[1024,1024]{1,0:T(8,128)(2,1)}, u32[]{:S(2)}, u32[]{:S(2)}) collective-permute-start(bf16[1024,1024]{1,0:T(8,128)(2,1)} %back_rows.2), channel_id=1, source_target_pairs={{0,1},{1,0},{2,3},{3,2},{4,5},{5,4},{6,7},{7,6},{8,9},{9,8},{10,11... | collective-permute-start | bytes 6291464 | tf_op jit(solution)/shard_map/ppermute | solution.py:970
  196.8 15.5 %collective-permute-start.11 = (bf16[4,136,512]{2,1,0:T(8,128)(2,1)S(1)}, bf16[4,136,512]{2,1,0:T(8,128)(2,1)S(1)}, u32[]{:S(2)}, u32[]{:S(2)}) collective-permute-start(bf16[4,136,512]{2,1,0:T(8,128)(2,1)S(1)} %get-tuple-element.156), channel_id=1, source_target_pairs={{0,2},{2,0},{4,6},{6,4},{8,10},{10,8},{12,14},{14,12},{16,18},{18,... | collective-permute-start | bytes 1671176 | tf_op jit(solution)/shard_map/ppermute | solution.py:904
  198.2 14.1 %collective-permute-start.10 = (bf16[4,128,512]{2,1,0:T(8,128)(2,1)S(1)}, bf16[4,128,512]{2,1,0:T(8,128)(2,1)S(1)}, u32[]{:S(2)}, u32[]{:S(2)}) collective-permute-start(bf16[4,128,512]{2,1,0:T(8,128)(2,1)S(1)} %get-tuple-element.155), channel_id=1, source_target_pairs={{0,4},{2,6},{4,0},{6,2},{8,12},{10,14},{12,8},{14,10},{16,20},{18,... | collective-permute-start | bytes 1572872 | tf_op jit(solution)/shard_map/ppermute | solution.py:904
  212.3 25.0 %collective-permute-start.14 = (bf16[1024,1024]{1,0:T(8,128)(2,1)}, bf16[1024,1024]{1,0:T(8,128)(2,1)}, u32[]{:S(2)}, u32[]{:S(2)}) collective-permute-start(bf16[1024,1024]{1,0:T(8,128)(2,1)} %out_rows.2), channel_id=1, source_target_pairs={{0,1},{1,0},{2,3},{3,2},{4,5},{5,4},{6,7},{7,6},{8,9},{9,8},{10,11... | collective-permute-start | bytes 6291464 | tf_op jit(solution)/shard_map/ppermute | solution.py:970
  212.7 18.8 %collective-permute-start.13 = (bf16[2,264,512]{2,1,0:T(8,128)(2,1)S(1)}, bf16[2,264,512]{2,1,0:T(8,128)(2,1)S(1)}, u32[]{:S(2)}, u32[]{:S(2)}) collective-permute-start(bf16[2,264,512]{2,1,0:T(8,128)(2,1)S(1)} %pad_maximum_fusion.2), channel_id=1, source_target_pairs={{0,8},{2,10},{4,12},{6,14},{8,0},{10,2},{12,4},{14,6},{16,24},{18,... | collective-permute-start | bytes 1622024 | tf_op jit(solution)/shard_map/ppermute | solution.py:904
  232.4 3.0 %collective-permute-start.17 = (f32[2,32,1024]{2,1,0:T(8,128)S(1)}, f32[2,32,1024]{2,1,0:T(8,128)S(1)}, u32[]{:S(2)}, u32[]{:S(2)}) collective-permute-start(f32[2,32,1024]{2,1,0:T(8,128)S(1)} %dynamic-slice_bitcast_fusion), channel_id=1, source_target_pairs={{0,1},{1,0},{2,3},{3,2},{4,5},{5,4},{6,7},{7,6},{8,9},{9,8},{10,11... | collective-permute-start | bytes 786440 | tf_op jit(solution)/shard_map/ppermute | solution.py:970
  232.8 17.1 %collective-permute-start.15 = (bf16[1,264,512]{2,1,0:T(8,128)(2,1)S(1)}, bf16[1,264,512]{2,1,0:T(8,128)(2,1)S(1)}, u32[]{:S(2)}, u32[]{:S(2)}) collective-permute-start(bf16[1,264,512]{2,1,0:T(8,128)(2,1)S(1)} %get-tuple-element.167), channel_id=1, source_target_pairs={{0,16},{2,18},{4,20},{6,22},{8,24},{10,26},{12,28},{14,30},{16,0},... | collective-permute-start | bytes 811016 | tf_op jit(solution)/shard_map/ppermute | solution.py:904
  237.2 16.5 %copy-start.2 = (f32[32,4096]{1,0:T(8,128)}, f32[32,4096]{1,0:T(8,128)S(1)}, u32[]{:S(2)}) copy-start(f32[32,4096]{1,0:T(8,128)S(1)} %reshape.98) | copy-start | bytes 1572868
  250.2 10.3 %collective-permute-start.16 = (f32[104,512]{1,0:T(8,128)S(1)}, f32[104,512]{1,0:T(8,128)S(1)}, u32[]{:S(2)}, u32[]{:S(2)}) collective-permute-start(f32[104,512]{1,0:T(8,128)S(1)} %pad_maximum_fusion.5), channel_id=1, source_target_pairs={{0,1},{1,0},{2,3},{3,2},{4,5},{5,4},{6,7},{7,6},{8,9},{9,8},{10,11... | collective-permute-start | bytes 638984 | tf_op jit(solution)/shard_map/ppermute | solution.py:970
  250.3 10.2 %collective-permute-start.18 = (f32[32,1024]{1,0:T(8,128)S(1)}, f32[32,1024]{1,0:T(8,128)S(1)}, u32[]{:S(2)}, u32[]{:S(2)}) collective-permute-start(f32[32,1024]{1,0:T(8,128)S(1)} %pad_maximum_fusion.6), channel_id=1, source_target_pairs={{0,0},{1,16},{2,1},{3,17},{4,2},{5,18},{6,3},{7,19},{8,4},{9,20},{... | collective-permute-start | bytes 393224 | tf_op jit(solution)/shard_map/ppermute | solution.py:1076
  260.6 5.6 %copy-start.10 = (f32[32]{0:T(128)}, f32[32]{0:T(128)S(1)}, u32[]{:S(2)}) copy-start(f32[32]{0:T(128)S(1)} %fusion.16) | copy-start | bytes 388
  261.3 4.9 %copy-start.5 = (f32[32,3072]{1,0:T(8,128)}, f32[32,3072]{1,0:T(8,128)S(1)}, u32[]{:S(2)}) copy-start(f32[32,3072]{1,0:T(8,128)S(1)} %fusion.2) | copy-start | bytes 1179652

commit v3 on v2

--- a/solution.py
+++ b/solution.py
@@ -507,7 +507,7 @@
         back_low = back.astype(BF)
         scale_grad[:, cols] += jnp.sum(back, axis=0, keepdims=True)
         yield
-        dt = mm(back_low, mix_high[...], NT) + mm(back_low, mix_low[...], NT)
+        dt = mm(back_low, mix_high[...], NT)
         dt = dt - mm(back_low, ones) * turned[0, g][rows] * (HEAD ** (-0.5))
         yield
         out = turn(dt, cosine[rows], -low[rows], -high[rows]).astype(BF)
@@ -524,9 +524,9 @@
         def _(j):
             strip_copy(info[0], w_up, up_buf, sems, 0, j).wait()
 
-        @pl.loop(0, upb.shape[1] // GROUP)
+        @pl.loop(0, upb.shape[1] // (2 * GROUP))
         def _(j):
-            cols = pl.ds(pl.multiple_of(j * GROUP, GROUP), GROUP)
+            cols = pl.ds(pl.multiple_of(j * 2 * GROUP, GROUP), 2 * GROUP)
             shift[...] += exact_row(upb[:, cols], up_buf[:, cols])
 
 
@@ -583,7 +583,7 @@
         dv[rows, cols] = dvc
         bias_v[:, cols] += jnp.sum(dvc.astype(F32), axis=0, keepdims=True)
         yield
-        dt = mm(back_low, mix_high[...], NT) + mm(back_low, mix_low[...], NT)
+        dt = mm(back_low, mix_high[...], NT)
         dt = dt - mm(back_low, ones) * tk_s[rows, cols].astype(F32) * (HEAD ** (-0.5))
         yield
         out = turn(dt, cosine[rows], -low[rows], -high[rows]).astype(BF)

time: 267 us -> 267 us (level)
  waiting for transfers between devices: 12.5 us -> 16.1 us
    ppermute x12, waiting for transfers between devices: 6.84 us -> 9.75 us  [cross(): return lax.ppermute(value, 'dp', [(i, i ^ bit) for i in range(ndp)])]
  transfers between devices with their start and end apart: 19 -> 19, of which waited for: 8 -> 9; matrix products, arithmetic and copies ran while one was open for 3% -> 3% of each run, Pallas kernels for 62% -> 61%
where the time goes in v3:
time: 267 us
  Pallas kernels  209 us (78%)
  starting transfers between devices  20.2 us (8%)
  waiting for transfers between devices  16.1 us (6%)
  other arithmetic  12.9 us (5%)
  local copies, waits for them, and re-layouts  6.97 us (3%)
    pallas_call x1, Pallas kernels, attention_front(): pl.pallas_call(attn_front_kernel, out_shape=(*(jax.ShapeDtypeStruct((tota...  44.3 us
    pallas_call x2, Pallas kernels, mlp_rows(): pl.pallas_call(partial(mlp_kernel, half, tiles), out_shape=outs, grid_spe...  43.6 us
    pallas_call x2, Pallas kernels, back_rows(): pl.pallas_call(partial(back_kernel, own), out_shape=jax.ShapeDtypeStruct(...  32.5 us
    pallas_call x1, Pallas kernels, mlp_weight_grads(): pl.pallas_call(partial(mlp_grad_kernel, tiles), out_shape=(shape,) * 4, g...  24.6 us
    pallas_call x2, Pallas kernels, out_rows(): pl.pallas_call(partial(out_kernel, own), out_shape=jax.ShapeDtypeStruct((...  24.5 us
    pallas_call x1, Pallas kernels, attention_rear(): pl.pallas_call(partial(attn_rear_kernel, tiles), out_shape=(*(jax.ShapeDt...  20.4 us
    pallas_call x1, Pallas kernels, attn_weight_grads(): pl.pallas_call(attn_grad_kernel, out_shape=(shapes[0], shapes[0], shapes[...  16.8 us
    ppermute x12, starting transfers between devices, cross(): return lax.ppermute(value, 'dp', [(i, i ^ bit) for i in range(ndp)])  16.2 us
  transfers between devices with their start and end apart: 19, of which 9 were waited for; matrix products, arithmetic and copies ran while one was open for 3% of the time, Pallas kernels for 61%

profile of v3, /device:TPU:10, one launch (start us, length us, event | category | flops | bytes accessed | tf_op | source)
XLA Modules:
  0.0 266.6 jit_solution(2464587079942811994)
XLA Ops:
  0.7 0.5 collective-permute-start.1
  1.9 1.9 prepare.1
  3.7 0.6 pad_add_fusion.1.info
  4.3 0.6 pad_add_fusion.table
  4.9 21.8 %mlp_rows.2 = (bf16[2048,1024]{1,0:T(8,128)(2,1)}, bf16[2048,1024]{1,0:T(8,128)(2,1)}, bf16[2048,2048]{1,0:T(8,128)(2,1)}, bf16[2048,2048]{1,0:T(8,128)(2,1)}, f32[1,2048]{1,0:T(1,128)}, /*index=5*/f32[1,1024]{1,0:T(1,128)}) custom-call(s32[3]{0:T(128)} %pad_add_fusion.1.info, bf16[1024,1024]{1,0:T(8,128)(2,1)} %rest_0_.3, bf16[1024,1024]{1,0:T(8,128)(2,1)} %cot.1, ...), custom_call_target="tpu_custom_call" | custom-call | flops 3435973888 | bytes 18454936 | tf_op jit(solution)/shard_map/mlp_rows/pallas_call | solution.py:177
  26.7 21.8 %mlp_rows.3 = (bf16[2048,1024]{1,0:T(8,128)(2,1)}, bf16[2048,1024]{1,0:T(8,128)(2,1)}, bf16[2048,2048]{1,0:T(8,128)(2,1)}, bf16[2048,2048]{1,0:T(8,128)(2,1)}, f32[1,2048]{1,0:T(1,128)}, /*index=5*/f32[1,1024]{1,0:T(1,128)}) custom-call(s32[3]{0:T(128)} %pad_add_fusion.1.info, ...), custom_call_target="tpu_custom_call", output_to_operand_aliasing={{0}: (8, {}), {1}: (9, {}), {2}: (10, {}), {3}: (11, {})} | custom-call | flops 3435973888 | bytes 18454936 | tf_op jit(solution)/shard_map/mlp_rows/pallas_call | solution.py:177
  48.6 24.6 %mlp_weight_grads.1 = (bf16[8,128,1024]{2,1,0:T(8,128)(2,1)}, bf16[8,128,1024]{2,1,0:T(8,128)(2,1)}, bf16[8,128,1024]{2,1,0:T(8,128)(2,1)}, bf16[8,128,1024]{2,1,0:T(8,128)(2,1)}) custom-call(s32[2,16]{1,0:T(2,128)} %pad_add_fusion.table, bf16[2048,2048]{1,0:T(8,128)(2,1)} %get-tuple-element.100.act, bf16[2048,1024]{1,0:T(8,128)(2,1)} %get-tuple-element.101.target.rest_2_, ...), custom_call_target="tpu_custom_call" | custom-call | flops 6871947776 | bytes 13421772 | tf_op jit(solution)/shard_map/mlp_weight_grads/pallas_call | solution.py:285
  73.2 0.6 collective-permute-start.2
  73.8 1.5 collective-permute-start.3
  75.3 44.3 %attention_front.1 = (bf16[2048,512]{1,0:T(8,128)(2,1)}, bf16[2048,512]{1,0:T(8,128)(2,1)}, bf16[2048,512]{1,0:T(8,128)(2,1)}, bf16[2048,512]{1,0:T(8,128)(2,1)}...) custom-call(s32[3]{0:T(128)} %pad_add_fusion.1.info, ...), custom_call_target="tpu_custom_call" | custom-call | flops 10307921920 | bytes 10066329 | tf_op jit(solution)/shard_map/attention_front/pallas_call | solution.py:671
  119.6 1.5 collective-permute-done.2
  121.1 0.2 collective-permute-done.3
  121.3 1.9 add_convert_fusion
  123.2 2.0 add_convert_fusion.2
  125.2 1.5 collective-permute-start.4
  126.7 1.5 collective-permute-start.5
  128.5 20.4 %attention_rear.1 = (bf16[2048,512]{1,0:T(8,128)(2,1)}, bf16[2048,512]{1,0:T(8,128)(2,1)}, f32[4,512]{1,0:T(4,128)}, f32[1,1024]{1,0:T(1,128)}) custom-call(s32[3]{0:T(128)} %pad_add_fusion.1.info, bf16[2048,512]{1,0:T(8,128)(2,1)} %get-tuple-element.116.fq_s, bf16[2048,512]{1,0:T(8,128)(2,1)} %get-tuple-element.117.fk_s, ...), custom_call_target="tpu_custom_call" | custom-call | flops 5153960960 | bytes 6710886 | tf_op jit(solution)/shard_map/attention_rear/pallas_call | solution.py:719
  148.9 0.7 collective-permute-done.4
  149.6 1.2 collective-permute-done.5
  150.8 1.6 add_convert_fusion.11
  152.4 0.4 add_convert_fusion.10
  152.9 0.5 collective-permute-start.6
  153.9 0.7 copy.55
  154.6 16.8 %attn_weight_grads.1 = (bf16[8,128,512]{2,1,0:T(8,128)(2,1)}, bf16[8,128,512]{2,1,0:T(8,128)(2,1)}, bf16[8,136,512]{2,1,0:T(8,128)(2,1)}, bf16[8,136,512]{2,1,0:T(8,128)(2,1)}) custom-call(s32[2,16]{1,0:T(2,128)} %pad_add_fusion.table, bf16[2048,1024]{1,0:T(8,128)(2,1)} %get-tuple-element.102.normed, bf16[2048,512]{1,0:T(8,128)(2,1)} %get-tuple-element.135.attended, ...), custom_call_target="tpu_custom_call" | custom-call | flops 3435973888 | bytes 8388608 | tf_op jit(solution)/shard_map/attn_weight_grads/pallas_call | solution.py:349
  171.5 0.7 collective-permute-start.8
  172.2 1.4 collective-permute-start.7
  173.5 2.5 collective-permute-done.6
  176.0 0.4 add_convert_fusion.8
  176.4 2.6 collective-permute-start.9
  179.0 15.0 %back_rows.2 = bf16[1024,1024]{1,0:T(8,128)(2,1)} custom-call(s32[3]{0:T(128)} %pad_add_fusion.1.info, bf16[2048,512]{1,0:T(8,128)(2,1)} %get-tuple-element.136.dq, bf16[2048,512]{1,0:T(8,128)(2,1)} %get-tuple-element.137.dk, bf16[2048,512]{1,0:T(8,128)(2,1)} %get-tuple-element.138.dv, bf16[2048,2048]{1,0:T(8,128)(2,1)} %get-tuple-element.103.up_grad, ...), custom_call_target="tpu_custom_call" | custom-call | flops 3006477056 | bytes 8388608 | tf_op jit(solution)/shard_map/back_rows/pallas_call | solution.py:860
  194.0 1.0 collective-permute-done.7
  195.0 1.1 collective-permute-done.8
  196.2 0.3 add_convert_fusion.4
  196.5 0.3 add_convert_fusion.6
  196.8 1.4 collective-permute-start.11
  198.2 0.5 collective-permute-start.10
  198.8 11.8 %out_rows.2 = bf16[1024,1024]{1,0:T(8,128)(2,1)} custom-call(s32[3]{0:T(128)} %pad_add_fusion.1.info, bf16[2048,2048]{1,0:T(8,128)(2,1)} %get-tuple-element.100.act, bf16[2048,512]{1,0:T(8,128)(2,1)} %get-tuple-element.135.attended, bf16[1024,1024]{1,0:T(8,128)(2,1)} %w_proj.5, bf16[4096,1024]{1,0:T(8,128)(2,1)} %w_down.7), custom_call_target="tpu_custom_call" | custom-call | flops 2147483648 | bytes 5033164 | tf_op jit(solution)/shard_map/out_rows/pallas_call | solution.py:780
  210.6 0.2 add_bitcast_fusion
  210.8 1.5 collective-permute-done.10
  212.3 0.1 add_convert_fusion.18
  212.4 0.1 add_convert_fusion.14
  212.7 1.4 collective-permute-start.13
  214.0 17.4 %back_rows.3 = f32[1024,1024]{1,0:T(8,128)} custom-call(s32[3]{0:T(128)} %pad_add_fusion.1.info, bf16[2048,512]{1,0:T(8,128)(2,1)} %get-tuple-element.136.dq, bf16[2048,512]{1,0:T(8,128)(2,1)} %get-tuple-element.137.dk, bf16[2048,512]{1,0:T(8,128)(2,1)} %get-tuple-element.138.dv, bf16[2048,2048]{1,0:T(8,128)(2,1)} %get-tuple-element.103.up_grad, ...), custom_call_target="tpu_custom_call" | custom-call | flops 3006477056 | bytes 8388608 | tf_op jit(solution)/shard_map/back_rows/pallas_call | solution.py:860
  231.5 0.9 fusion.21
  232.4 0.3 collective-permute-start.17
  232.7 0.1 add_convert_fusion.16
  232.8 2.6 collective-permute-start.15
  235.5 0.2 copy.48
  235.7 0.2 reshape.96
  235.9 0.2 copy.49
  236.1 0.2 reshape.97
  236.4 0.4 copy.50
  236.8 0.4 reshape.98
  237.3 12.7 %out_rows.3 = bf16[1024,1024]{1,0:T(8,128)(2,1)} custom-call(s32[3]{0:T(128)} %pad_add_fusion.1.info, bf16[2048,2048]{1,0:T(8,128)(2,1)} %get-tuple-element.100.act, bf16[2048,512]{1,0:T(8,128)(2,1)} %get-tuple-element.135.attended, bf16[1024,1024]{1,0:T(8,128)(2,1)} %w_proj.5, bf16[4096,1024]{1,0:T(8,128)(2,1)} %w_down.7, bf16[1024,1024]{1,0:T(8,128)(2,1)} %rest_0_.3, ...), custom_call_target="tpu_custom_call" | custom-call | flops 2147483648 | bytes 5033164 | tf_op jit(solution)/shard_map/out_rows/pallas_call | solution.py:780
  250.3 3.1 %collective-permute-start.18 = (f32[32,1024]{1,0:T(8,128)S(1)}, f32[32,1024]{1,0:T(8,128)S(1)}, u32[]{:S(2)}, u32[]{:S(2)}) collective-permute-start(f32[32,1024]{1,0:T(8,128)S(1)} %pad_maximum_fusion.6), channel_id=1, source_target_pairs={{0,0},{1,16},{2,1},{3,17},{4,2},{5,18},{6,3},{7,19},{8,4},{9,20},{... | collective-permute-start | bytes 393224 | tf_op jit(solution)/shard_map/ppermute | solution.py:1076
  253.4 1.1 multiply_reduce_fusion
  254.5 6.3 %collective-permute-done.18 = f32[32,1024]{1,0:T(8,128)S(1)} collective-permute-done((f32[32,1024]{1,0:T(8,128)S(1)}, f32[32,1024]{1,0:T(8,128)S(1)}, u32[]{:S(2)}, u32[]{:S(2)}) %collective-permute-start.18) | collective-permute-done | bytes 131104 | tf_op jit(solution)/shard_map/ppermute | solution.py:1076
  261.0 0.5 fusion.17
  261.7 1.2 multiply_reduce_fusion.1
  263.1 0.5 fusion.15
  263.6 0.5 fusion.18
  264.1 1.3 convert_divide_fusion
  265.4 0.5 copy.70
  265.9 0.7 copy.71
  (83 shorter events, 1.8 us)
Async XLA Ops:
  0.6 26.1 %collective-permute-start = (bf16[1024,1024]{1,0:T(8,128)(2,1)}, bf16[1024,1024]{1,0:T(8,128)(2,1)}, u32[]{:S(2)}, u32[]{:S(2)}) collective-permute-start(bf16[1024,1024]{1,0:T(8,128)(2,1)} %rest_0_.3), channel_id=1, source_target_pairs={{0,1},{1,0},{2,3},{3,2},{4,5},{5,4},{6,7},{7,6},{8,9},{9,8},{10,11... | collective-permute-start | bytes 6291464 | tf_op jit(solution)/shard_map/ppermute | solution.py:970
  0.7 26.0 %collective-permute-start.1 = (bf16[1024,1024]{1,0:T(8,128)(2,1)}, bf16[1024,1024]{1,0:T(8,128)(2,1)}, u32[]{:S(2)}, u32[]{:S(2)}) collective-permute-start(bf16[1024,1024]{1,0:T(8,128)(2,1)} %cot.1), channel_id=1, source_target_pairs={{0,1},{1,0},{2,3},{3,2},{4,5},{5,4},{6,7},{7,6},{8,9},{9,8},{10,11... | collective-permute-start | bytes 6291464 | tf_op jit(solution)/shard_map/ppermute | solution.py:970
  73.2 47.9 %collective-permute-start.2 = (bf16[8,128,1024]{2,1,0:T(8,128)(2,1)}, bf16[8,128,1024]{2,1,0:T(8,128)(2,1)S(1)}, u32[]{:S(2)}, u32[]{:S(2)}) collective-permute-start(bf16[8,128,1024]{2,1,0:T(8,128)(2,1)} %get-tuple-element.109), channel_id=1, source_target_pairs={{0,2},{2,0},{4,6},{6,4},{8,10},{10,8},{12,14},{14,12},{16,18},{18,... | collective-permute-start | bytes 6291464 | tf_op jit(solution)/shard_map/ppermute | solution.py:904
  73.8 47.5 %collective-permute-start.3 = (bf16[8,128,1024]{2,1,0:T(8,128)(2,1)}, bf16[8,128,1024]{2,1,0:T(8,128)(2,1)S(1)}, u32[]{:S(2)}, u32[]{:S(2)}) collective-permute-start(bf16[8,128,1024]{2,1,0:T(8,128)(2,1)} %get-tuple-element.110), channel_id=1, source_target_pairs={{0,4},{2,6},{4,0},{6,2},{8,12},{10,14},{12,8},{14,10},{16,20},{18,... | collective-permute-start | bytes 6291464 | tf_op jit(solution)/shard_map/ppermute | solution.py:904
  75.3 46.0 %copy-start.1 = (bf16[8,128,1024]{2,1,0:T(8,128)(2,1)S(1)}, bf16[8,128,1024]{2,1,0:T(8,128)(2,1)}, u32[]{:S(2)}) copy-start(bf16[8,128,1024]{2,1,0:T(8,128)(2,1)} %get-tuple-element.112) | copy-start | bytes 6291460
  121.3 1.9 copy-start
  123.2 5.0 %copy-start.8 = (f32[1,1024]{1,0:T(1,128)S(1)}, f32[1,1024]{1,0:T(1,128)}, u32[]{:S(2)}) copy-start(f32[1,1024]{1,0:T(1,128)} %get-tuple-element.141) | copy-start | bytes 12292
  123.2 5.2 %copy-start.6 = (f32[1,2048]{1,0:T(1,128)S(1)}, f32[1,2048]{1,0:T(1,128)}, u32[]{:S(2)}) copy-start(f32[1,2048]{1,0:T(1,128)} %get-tuple-element.107.upb) | copy-start | bytes 24580
  125.2 24.4 %collective-permute-start.4 = (bf16[4,128,1024]{2,1,0:T(8,128)(2,1)}, bf16[4,128,1024]{2,1,0:T(8,128)(2,1)}, u32[]{:S(2)}, u32[]{:S(2)}) collective-permute-start(bf16[4,128,1024]{2,1,0:T(8,128)(2,1)} %get-tuple-element.126), channel_id=1, source_target_pairs={{0,4},{2,6},{4,0},{6,2},{8,12},{10,14},{12,8},{14,10},{16,20},{18,... | collective-permute-start | bytes 3145736 | tf_op jit(solution)/shard_map/ppermute | solution.py:904
  126.7 24.0 %collective-permute-start.5 = (bf16[4,128,1024]{2,1,0:T(8,128)(2,1)}, bf16[4,128,1024]{2,1,0:T(8,128)(2,1)S(1)}, u32[]{:S(2)}, u32[]{:S(2)}) collective-permute-start(bf16[4,128,1024]{2,1,0:T(8,128)(2,1)} %get-tuple-element.127), channel_id=1, source_target_pairs={{0,2},{2,0},{4,6},{6,4},{8,10},{10,8},{12,14},{14,12},{16,18},{18,... | collective-permute-start | bytes 3145736 | tf_op jit(solution)/shard_map/ppermute | solution.py:904
  152.8 0.7 copy-start.7
  152.8 1.0 copy-start.9
  152.9 23.1 %collective-permute-start.6 = (bf16[2,256,1024]{2,1,0:T(8,128)(2,1)S(1)}, bf16[2,256,1024]{2,1,0:T(8,128)(2,1)S(1)}, u32[]{:S(2)}, u32[]{:S(2)}) collective-permute-start(bf16[2,256,1024]{2,1,0:T(8,128)(2,1)S(1)} %pad_maximum_fusion), channel_id=1, source_target_pairs={{0,8},{2,10},{4,12},{6,14},{8,0},{10,2},{12,4},{14,6},{16,24},{18,... | collective-permute-start | bytes 3145736 | tf_op jit(solution)/shard_map/ppermute | solution.py:904
  171.5 24.7 %collective-permute-start.8 = (bf16[8,136,512]{2,1,0:T(8,128)(2,1)}, bf16[8,136,512]{2,1,0:T(8,128)(2,1)S(1)}, u32[]{:S(2)}, u32[]{:S(2)}) collective-permute-start(bf16[8,136,512]{2,1,0:T(8,128)(2,1)} %get-tuple-element.144), channel_id=1, source_target_pairs={{0,4},{2,6},{4,0},{6,2},{8,12},{10,14},{12,8},{14,10},{16,20},{18,... | collective-permute-start | bytes 3342344 | tf_op jit(solution)/shard_map/ppermute | solution.py:904
  172.2 22.9 %collective-permute-start.7 = (bf16[8,128,512]{2,1,0:T(8,128)(2,1)}, bf16[8,128,512]{2,1,0:T(8,128)(2,1)S(1)}, u32[]{:S(2)}, u32[]{:S(2)}) collective-permute-start(bf16[8,128,512]{2,1,0:T(8,128)(2,1)} %get-tuple-element.143), channel_id=1, source_target_pairs={{0,2},{2,0},{4,6},{6,4},{8,10},{10,8},{12,14},{14,12},{16,18},{18,... | collective-permute-start | bytes 3145736 | tf_op jit(solution)/shard_map/ppermute | solution.py:904
  176.4 19.8 %copy-start.3 = (bf16[8,136,512]{2,1,0:T(8,128)(2,1)S(1)}, bf16[8,136,512]{2,1,0:T(8,128)(2,1)}, u32[]{:S(2)}) copy-start(bf16[8,136,512]{2,1,0:T(8,128)(2,1)} %get-tuple-element.146) | copy-start | bytes 3342340
  176.4 34.2 %collective-permute-start.9 = (bf16[1,256,1024]{2,1,0:T(8,128)(2,1)S(1)}, bf16[1,256,1024]{2,1,0:T(8,128)(2,1)S(1)}, u32[]{:S(2)}, u32[]{:S(2)}) collective-permute-start(bf16[1,256,1024]{2,1,0:T(8,128)(2,1)S(1)} %get-tuple-element.150), channel_id=1, source_target_pairs={{0,16},{2,18},{4,20},{6,22},{8,24},{10,26},{12,28},{14,30},{16,0},... | collective-permute-start | bytes 1572872 | tf_op jit(solution)/shard_map/ppermute | solution.py:904
  194.0 2.5 copy-start.4
  196.2 17.9 %collective-permute-start.12 = (bf16[1024,1024]{1,0:T(8,128)(2,1)}, bf16[1024,1024]{1,0:T(8,128)(2,1)}, u32[]{:S(2)}, u32[]{:S(2)}) collective-permute-start(bf16[1024,1024]{1,0:T(8,128)(2,1)} %back_rows.2), channel_id=1, source_target_pairs={{0,1},{1,0},{2,3},{3,2},{4,5},{5,4},{6,7},{7,6},{8,9},{9,8},{10,11... | collective-permute-start | bytes 6291464 | tf_op jit(solution)/shard_map/ppermute | solution.py:970
  196.8 15.5 %collective-permute-start.11 = (bf16[4,136,512]{2,1,0:T(8,128)(2,1)S(1)}, bf16[4,136,512]{2,1,0:T(8,128)(2,1)S(1)}, u32[]{:S(2)}, u32[]{:S(2)}) collective-permute-start(bf16[4,136,512]{2,1,0:T(8,128)(2,1)S(1)} %get-tuple-element.156), channel_id=1, source_target_pairs={{0,2},{2,0},{4,6},{6,4},{8,10},{10,8},{12,14},{14,12},{16,18},{18,... | collective-permute-start | bytes 1671176 | tf_op jit(solution)/shard_map/ppermute | solution.py:904
  198.2 14.1 %collective-permute-start.10 = (bf16[4,128,512]{2,1,0:T(8,128)(2,1)S(1)}, bf16[4,128,512]{2,1,0:T(8,128)(2,1)S(1)}, u32[]{:S(2)}, u32[]{:S(2)}) collective-permute-start(bf16[4,128,512]{2,1,0:T(8,128)(2,1)S(1)} %get-tuple-element.155), channel_id=1, source_target_pairs={{0,4},{2,6},{4,0},{6,2},{8,12},{10,14},{12,8},{14,10},{16,20},{18,... | collective-permute-start | bytes 1572872 | tf_op jit(solution)/shard_map/ppermute | solution.py:904
  212.3 25.0 %collective-permute-start.14 = (bf16[1024,1024]{1,0:T(8,128)(2,1)}, bf16[1024,1024]{1,0:T(8,128)(2,1)}, u32[]{:S(2)}, u32[]{:S(2)}) collective-permute-start(bf16[1024,1024]{1,0:T(8,128)(2,1)} %out_rows.2), channel_id=1, source_target_pairs={{0,1},{1,0},{2,3},{3,2},{4,5},{5,4},{6,7},{7,6},{8,9},{9,8},{10,11... | collective-permute-start | bytes 6291464 | tf_op jit(solution)/shard_map/ppermute | solution.py:970
  212.7 18.8 %collective-permute-start.13 = (bf16[2,264,512]{2,1,0:T(8,128)(2,1)S(1)}, bf16[2,264,512]{2,1,0:T(8,128)(2,1)S(1)}, u32[]{:S(2)}, u32[]{:S(2)}) collective-permute-start(bf16[2,264,512]{2,1,0:T(8,128)(2,1)S(1)} %pad_maximum_fusion.2), channel_id=1, source_target_pairs={{0,8},{2,10},{4,12},{6,14},{8,0},{10,2},{12,4},{14,6},{16,24},{18,... | collective-permute-start | bytes 1622024 | tf_op jit(solution)/shard_map/ppermute | solution.py:904
  232.4 3.0 %collective-permute-start.17 = (f32[2,32,1024]{2,1,0:T(8,128)S(1)}, f32[2,32,1024]{2,1,0:T(8,128)S(1)}, u32[]{:S(2)}, u32[]{:S(2)}) collective-permute-start(f32[2,32,1024]{2,1,0:T(8,128)S(1)} %dynamic-slice_bitcast_fusion), channel_id=1, source_target_pairs={{0,1},{1,0},{2,3},{3,2},{4,5},{5,4},{6,7},{7,6},{8,9},{9,8},{10,11... | collective-permute-start | bytes 786440 | tf_op jit(solution)/shard_map/ppermute | solution.py:970
  232.8 17.1 %collective-permute-start.15 = (bf16[1,264,512]{2,1,0:T(8,128)(2,1)S(1)}, bf16[1,264,512]{2,1,0:T(8,128)(2,1)S(1)}, u32[]{:S(2)}, u32[]{:S(2)}) collective-permute-start(bf16[1,264,512]{2,1,0:T(8,128)(2,1)S(1)} %get-tuple-element.167), channel_id=1, source_target_pairs={{0,16},{2,18},{4,20},{6,22},{8,24},{10,26},{12,28},{14,30},{16,0},... | collective-permute-start | bytes 811016 | tf_op jit(solution)/shard_map/ppermute | solution.py:904
  237.2 16.2 %copy-start.2 = (f32[32,4096]{1,0:T(8,128)}, f32[32,4096]{1,0:T(8,128)S(1)}, u32[]{:S(2)}) copy-start(f32[32,4096]{1,0:T(8,128)S(1)} %reshape.98) | copy-start | bytes 1572868
  250.2 10.7 %collective-permute-start.16 = (f32[104,512]{1,0:T(8,128)S(1)}, f32[104,512]{1,0:T(8,128)S(1)}, u32[]{:S(2)}, u32[]{:S(2)}) collective-permute-start(f32[104,512]{1,0:T(8,128)S(1)} %pad_maximum_fusion.5), channel_id=1, source_target_pairs={{0,1},{1,0},{2,3},{3,2},{4,5},{5,4},{6,7},{7,6},{8,9},{9,8},{10,11... | collective-permute-start | bytes 638984 | tf_op jit(solution)/shard_map/ppermute | solution.py:970
  250.3 10.6 %collective-permute-start.18 = (f32[32,1024]{1,0:T(8,128)S(1)}, f32[32,1024]{1,0:T(8,128)S(1)}, u32[]{:S(2)}, u32[]{:S(2)}) collective-permute-start(f32[32,1024]{1,0:T(8,128)S(1)} %pad_maximum_fusion.6), channel_id=1, source_target_pairs={{0,0},{1,16},{2,1},{3,17},{4,2},{5,18},{6,3},{7,19},{8,4},{9,20},{... | collective-permute-start | bytes 393224 | tf_op jit(solution)/shard_map/ppermute | solution.py:1076
  261.0 5.6 %copy-start.10 = (f32[32]{0:T(128)}, f32[32]{0:T(128)S(1)}, u32[]{:S(2)}) copy-start(f32[32]{0:T(128)S(1)} %fusion.16) | copy-start | bytes 388
  261.7 4.9 %copy-start.5 = (f32[32,3072]{1,0:T(8,128)}, f32[32,3072]{1,0:T(8,128)S(1)}, u32[]{:S(2)}) copy-start(f32[32,3072]{1,0:T(8,128)S(1)} %fusion.2) | copy-start | bytes 1179652
